TPU v7x, 32 devices: a whole 2x2x4 slice. The times are simulated.
32 devices in a mesh: shard: 8 (over z, y), seq: 4 (over x, core).
Axes of the slice: x: 2, y: 2, z: 4, core: 2. Of those that a mesh axis runs over, the one named last changes fastest.
Arguments:
- tokens: bfloat16 [16384, 768], P(('shard', 'seq')), may hold values from -6 to 6
- segment_ids: int32 [8, 2048], P('shard'), may hold values from 0 to 15, never falling along the last dimension, each value on 1 to 1024 neighbouring positions
- qkv_weight: bfloat16 [768, 2304], P('shard'), may hold values from -0.21875 to 0.21875
- out_weight: bfloat16 [768, 768], P('shard'), may hold values from -1.25 to 1.25
- up_weight: bfloat16 [768, 3072], P('shard'), may hold values from -0.21875 to 0.21875
- down_weight: bfloat16 [3072, 768], P('shard'), may hold values from -0.109375 to 0.109375
- first_gain: bfloat16 [768], P('shard'), may hold values from 0.5 to 1.5
- first_bias: bfloat16 [768], P('shard'), may hold values from -3 to 3
- second_gain: bfloat16 [768], P('shard'), may hold values from 0.5 to 1.5
- second_bias: bfloat16 [768], P('shard'), may hold values from -3 to 3
- out_grad: bfloat16 [16384, 768], P(('shard', 'seq')), may hold values from -6 to 6
Outputs:
- layer_output: bfloat16 [16384, 768], P(('shard', 'seq'))
- input_grad: float32 [16384, 768], P(('shard', 'seq'))
- qkv_grad: float32 [768, 2304], P('shard')
- mixer_grad: float32 [768, 768], P('shard')
- widen_grad: float32 [768, 3072], P('shard')
- narrow_grad: float32 [3072, 768], P('shard')
- first_gain_grad: float32 [768], P('shard')
- first_bias_grad: float32 [768], P('shard')
- second_gain_grad: float32 [768], P('shard')
- second_bias_grad: float32 [768], P('shard')
Inputs may be any that keep to these rules, and one draw needn't show every extreme that they name: `segment_ids`: in each row the ids never decrease; every document holds 1 to 1024 tokens and one holds exactly 1024.
All inputs are finite; a program needn't handle non-finite values.
Results may differ from a plain program's by a relative error of at most 0.02.
Values may be sent and summed in bfloat16 or wider, within the bound.
No kernel may reach another device: no remote copies, remote signals or barrier semaphores. Data moves between devices by JAX's collectives and lax.ppermute only.
A program may use at most 128 MiB of HBM per device.

v0:
```python
from functools import partial

import jax
import jax.numpy as jnp
from jax import lax
from jax.sharding import PartitionSpec as P

HEADS = 12
HEAD_DIM = 64


EPSILON = 1e-12
MASKED = -1000000000.0


def norm_rows(hidden, gain_vec, shift_vec):
    row_mean = jnp.mean(hidden, -1, keepdims=True)
    centred = hidden - row_mean
    variance = jnp.mean(centred * centred, -1, keepdims=True)
    inverse = lax.rsqrt(variance + EPSILON)
    normed = centred * inverse
    return (normed * gain_vec + shift_vec, normed, inverse)


def norm_back(grad_y, normed, inverse, gain_vec):
    grad_n = grad_y * gain_vec
    bracket = (
        grad_n
        - jnp.mean(grad_n, -1, keepdims=True)
        - normed * jnp.mean(grad_n * normed, -1, keepdims=True)
    )
    return (inverse * bracket, jnp.sum(grad_y * normed, 0), jnp.sum(grad_y, 0))


def contract_rows(left_mat, right_mat):
    return lax.dot_general(
        left_mat, right_mat, (((0,), (0,)), ((), ())), preferred_element_type=jnp.float32
    )


def contract_cols(left_mat, right_mat):
    return lax.dot_general(
        left_mat, right_mat, (((1,), (1,)), ((), ())), preferred_element_type=jnp.float32
    )


def split_heads(matrix):
    return matrix.reshape(matrix.shape[0], HEADS, HEAD_DIM).transpose(1, 0, 2)


def join_heads(matrix):
    return matrix.transpose(1, 0, 2).reshape(matrix.shape[1], HEADS * HEAD_DIM)


def forward(tokens, own_ids, all_ids, weights, second_pass):
    merged_full, mixer_full, widen_full, narrow_full, gain_one, bias_one, gain_two, bias_two = (
        weights
    )
    model_width = mixer_full.shape[0]
    merged_rows = jnp.dot(tokens, merged_full, preferred_element_type=jnp.float32).astype(
        jnp.bfloat16
    )
    key_value = merged_rows[:, model_width:]
    if second_pass:
        gathered = lax.all_gather(key_value, "seq", axis=0, tiled=True)
    else:
        gathered = lax.all_gather(key_value, "seq", axis=0, tiled=True)
    same_doc = own_ids[:, None] == all_ids[None, :]
    score_scale = HEAD_DIM ** (-0.5)

    def one_head(inputs):
        query, key_rows, value_rows = inputs
        scores = jnp.where(same_doc, contract_cols(query, key_rows) * score_scale, MASKED)
        maxima = jnp.max(scores, -1, keepdims=True)
        powers = jnp.exp(scores - maxima)
        totals = jnp.sum(powers, -1, keepdims=True)
        attend = (powers / totals).astype(jnp.bfloat16)
        return (
            jnp.dot(attend, value_rows, preferred_element_type=jnp.float32),
            (maxima + jnp.log(totals))[:, 0],
        )

    context, log_totals = lax.map(
        one_head,
        (
            split_heads(merged_rows[:, :model_width]),
            split_heads(gathered[:, :model_width]),
            split_heads(gathered[:, model_width:]),
        ),
    )
    context = join_heads(context).astype(jnp.bfloat16)
    attn_out = jnp.dot(context, mixer_full, preferred_element_type=jnp.float32)
    first_norm, normed_one, inverse_one = norm_rows(
        tokens.astype(jnp.float32) + attn_out,
        gain_one.astype(jnp.float32),
        bias_one.astype(jnp.float32),
    )
    first_low = first_norm.astype(jnp.bfloat16)
    pre_act = jnp.dot(first_low, widen_full, preferred_element_type=jnp.float32)
    act_low = jax.nn.gelu(pre_act, approximate=True).astype(jnp.bfloat16)
    mlp_out = jnp.dot(act_low, narrow_full, preferred_element_type=jnp.float32)
    result, normed_two, inverse_two = norm_rows(
        first_norm + mlp_out, gain_two.astype(jnp.float32), bias_two.astype(jnp.float32)
    )
    return (
        result,
        merged_rows,
        gathered,
        log_totals,
        context,
        normed_one,
        inverse_one,
        first_low,
        pre_act,
        act_low,
        normed_two,
        inverse_two,
    )


def shards(
    tokens,
    segment_ids,
    qkv_weight,
    out_weight,
    up_weight,
    down_weight,
    first_gain,
    first_bias,
    second_gain,
    second_bias,
    out_grad,
):
    local_rows = tokens.shape[0]
    all_ids = segment_ids[0]
    own_ids = lax.dynamic_slice_in_dim(all_ids, lax.axis_index("seq") * local_rows, local_rows)
    weights = (
        lax.all_gather(qkv_weight, "shard", axis=0, tiled=True),
        lax.all_gather(out_weight, "shard", axis=0, tiled=True),
        lax.all_gather(up_weight, "shard", axis=0, tiled=True),
        lax.all_gather(down_weight, "shard", axis=0, tiled=True),
        lax.all_gather(first_gain, "shard", axis=0, tiled=True),
        lax.all_gather(first_bias, "shard", axis=0, tiled=True),
        lax.all_gather(second_gain, "shard", axis=0, tiled=True),
        lax.all_gather(second_bias, "shard", axis=0, tiled=True),
    )
    stored = forward(tokens, own_ids, all_ids, weights, False)
    result = stored[0]
    weights = (
        lax.all_gather(qkv_weight, "shard", axis=0, tiled=True),
        lax.all_gather(out_weight, "shard", axis=0, tiled=True),
        lax.all_gather(up_weight, "shard", axis=0, tiled=True),
        lax.all_gather(down_weight, "shard", axis=0, tiled=True),
        lax.all_gather(first_gain, "shard", axis=0, tiled=True),
        lax.all_gather(first_bias, "shard", axis=0, tiled=True),
        lax.all_gather(second_gain, "shard", axis=0, tiled=True),
        lax.all_gather(second_bias, "shard", axis=0, tiled=True),
    )
    stored = forward(tokens, own_ids, all_ids, weights, True)
    merged_rows, gathered, log_totals, context = (stored[1], stored[2], stored[3], stored[4])
    normed_one, inverse_one, first_low, pre_act = (stored[5], stored[6], stored[7], stored[8])
    act_low, normed_two, inverse_two = (stored[9], stored[10], stored[11])
    merged_full, mixer_full, widen_full, narrow_full, gain_one, bias_one, gain_two, bias_two = (
        weights
    )
    model_width = mixer_full.shape[0]
    grad_two, late_gain, late_shift = norm_back(
        out_grad.astype(jnp.float32), normed_two, inverse_two, gain_two.astype(jnp.float32)
    )
    grad_mlp = grad_two.astype(jnp.bfloat16)
    grad_narrow = contract_rows(act_low, grad_mlp)
    grad_act = contract_cols(grad_mlp, narrow_full)
    unused, gelu_back = jax.vjp(partial(jax.nn.gelu, approximate=True), pre_act)
    grad_pre = gelu_back(grad_act)[0].astype(jnp.bfloat16)
    grad_widen = contract_rows(first_low, grad_pre)
    grad_first = grad_two + contract_cols(grad_pre, widen_full)
    grad_one, early_gain, early_shift = norm_back(
        grad_first, normed_one, inverse_one, gain_one.astype(jnp.float32)
    )
    grad_attn = grad_one.astype(jnp.bfloat16)
    grad_mixer = contract_rows(context, grad_attn)
    grad_context = contract_cols(grad_attn, mixer_full).astype(jnp.bfloat16)
    same_doc = own_ids[:, None] == all_ids[None, :]
    score_scale = HEAD_DIM ** (-0.5)
    query_heads = split_heads(merged_rows[:, :model_width])
    context_heads = split_heads(grad_context)

    def head_back(inputs):
        query, key_rows, value_rows, row_total, grad_head = inputs
        scores = jnp.where(same_doc, contract_cols(query, key_rows) * score_scale, MASKED)
        attend = jnp.exp(scores - row_total[:, None])
        grad_attend = contract_cols(grad_head, value_rows)
        grad_value = contract_rows(attend.astype(jnp.bfloat16), grad_head)
        row_term = jnp.sum(grad_attend * attend, -1, keepdims=True)
        grad_scores = (attend * (grad_attend - row_term)).astype(jnp.bfloat16)
        grad_query = (
            jnp.dot(grad_scores, key_rows, preferred_element_type=jnp.float32) * score_scale
        )
        grad_key = contract_rows(grad_scores, query) * score_scale
        return (grad_query, grad_key, grad_value)

    grad_query, grad_key, grad_value = lax.map(
        head_back,
        (
            query_heads,
            split_heads(gathered[:, :model_width]),
            split_heads(gathered[:, model_width:]),
            log_totals,
            context_heads,
        ),
    )
    key_part = jnp.concatenate([join_heads(grad_key), join_heads(grad_value)], 1)
    own_keys = lax.psum_scatter(
        key_part.astype(jnp.bfloat16), "seq", scatter_dimension=0, tiled=True
    ).astype(jnp.float32)
    grad_qkv = jnp.concatenate([join_heads(grad_query), own_keys], 1).astype(jnp.bfloat16)
    grad_merged = contract_rows(tokens, grad_qkv)
    grad_tokens = grad_one + contract_cols(grad_qkv, merged_full)
    shares = (
        lax.psum_scatter(
            grad_merged.astype(jnp.bfloat16), "shard", scatter_dimension=0, tiled=True
        ).astype(jnp.float32),
        lax.psum_scatter(
            grad_mixer.astype(jnp.bfloat16), "shard", scatter_dimension=0, tiled=True
        ).astype(jnp.float32),
        lax.psum_scatter(
            grad_widen.astype(jnp.bfloat16), "shard", scatter_dimension=0, tiled=True
        ).astype(jnp.float32),
        lax.psum_scatter(
            grad_narrow.astype(jnp.bfloat16), "shard", scatter_dimension=0, tiled=True
        ).astype(jnp.float32),
        lax.psum_scatter(
            early_gain.astype(jnp.bfloat16), "shard", scatter_dimension=0, tiled=True
        ).astype(jnp.float32),
        lax.psum_scatter(
            early_shift.astype(jnp.bfloat16), "shard", scatter_dimension=0, tiled=True
        ).astype(jnp.float32),
        lax.psum_scatter(
            late_gain.astype(jnp.bfloat16), "shard", scatter_dimension=0, tiled=True
        ).astype(jnp.float32),
        lax.psum_scatter(
            late_shift.astype(jnp.bfloat16), "shard", scatter_dimension=0, tiled=True
        ).astype(jnp.float32),
    )
    totals = (
        lax.psum(shares[0].astype(jnp.bfloat16), "seq").astype(jnp.float32),
        lax.psum(shares[1].astype(jnp.bfloat16), "seq").astype(jnp.float32),
        lax.psum(shares[2].astype(jnp.bfloat16), "seq").astype(jnp.float32),
        lax.psum(shares[3].astype(jnp.bfloat16), "seq").astype(jnp.float32),
        lax.psum(shares[4].astype(jnp.bfloat16), "seq").astype(jnp.float32),
        lax.psum(shares[5].astype(jnp.bfloat16), "seq").astype(jnp.float32),
        lax.psum(shares[6].astype(jnp.bfloat16), "seq").astype(jnp.float32),
        lax.psum(shares[7].astype(jnp.bfloat16), "seq").astype(jnp.float32),
    )
    return (
        result.astype(jnp.bfloat16),
        grad_tokens,
        totals[0],
        totals[1],
        totals[2],
        totals[3],
        totals[4],
        totals[5],
        totals[6],
        totals[7],
    )


def solution(mesh):
    placed = (
        P(("shard", "seq"), None),
        P("shard", None),
        P("shard", None),
        P("shard", None),
        P("shard", None),
        P("shard", None),
        P("shard"),
        P("shard"),
        P("shard"),
        P("shard"),
        P(("shard", "seq"), None),
    )
    return jax.shard_map(
        shards,
        mesh=mesh,
        in_specs=placed,
        out_specs=(
            P(("shard", "seq"), None),
            P(("shard", "seq"), None),
            P("shard", None),
            P("shard", None),
            P("shard", None),
            P("shard", None),
            P("shard"),
            P("shard"),
            P("shard"),
            P("shard"),
        ),
        check_vma=False,
    )
```

profile of v0, /device:TPU:0, one launch (start us, length us, event | category | flops | bytes accessed | tf_op | source)
XLA Modules:
  0.0 979.8 jit_solution(964042539213062995)
XLA Ops:
  8.0 70.2 %all-gather.6.cloned.1.call-done = bf16[768,2304]{1,0:T(8,128)(2,1)} async-done(((bf16[96,2304]{1,0:T(8,128)(2,1)}), bf16[768,2304]{1,0:T(8,128)(2,1)}) %all-gather.6.cloned.1.call-update) | async-done | bytes 3538960 | tf_op jit(solution)/shard_map/all_gather | solution.py:138
  78.1 4.2 convolution_convert_fusion.3
  87.8 19.3 %all-reduce.9 = (bf16[768]{0:T(1024)(128)(2,1)S(1)}, bf16[768]{0:T(1024)(128)(2,1)S(1)}, bf16[768]{0:T(1024)(128)(2,1)S(1)}) all-reduce(bf16[768]{0:T(1024)(128)(2,1)S(1)} %dynamic-update-slice.1, bf16[768]{0:T(1024)(128)(2,1)S(1)} %dynamic-update-slice, ...), channel_id=1, replica_groups=mesh['shard'=8,'seq'=4] {'shard'}, use_global_device_ids=true, to_apply=%add.1 | all-reduce | flops 2304 | bytes 9216
  109.0 19.8 %all-gather.8.cloned.1.call-done = bf16[2048,1536]{1,0:T(8,128)(2,1)} async-done(((bf16[512,1536]{1,0:T(8,128)(2,1)}), bf16[2048,1536]{1,0:T(8,128)(2,1)}) %all-gather.8.cloned.1.call-update) | async-done | bytes 6291472 | tf_op jit(solution)/shard_map/all_gather | solution.py:67
  128.9 4.9 fusion.122
  133.8 4.8 copy.42
  138.6 6.6 copy.45
  148.2 6.6 copy.46
  154.8 96.9 %while.40 = (s32[]{:T(128)}, bf16[12,512,64]{1,2,0:T(8,128)(2,1)S(1)}, f32[12,512]{1,0:T(8,128)S(1)}, bf16[12,512,64]{2,1,0:T(8,128)(2,1)}, bf16[12,2048,64]{2,1...) while((s32[]{:T(128)}, ...), condition=%wide.region_11.12_spmd.clone, body=%wide.region_8.11_spmd.clone.sunk | while | flops 277872128 | bytes 30703748 | solution.py:83
  159.6 3.3 fusion.176
  191.7 3.3 fusion.176
  207.8 3.9 fusion.176
  224.4 3.3 fusion.176
  254.8 7.0 fusion.116
  261.9 71.0 %all-gather.14.cloned.1.call-done = bf16[3072,768]{1,0:T(8,128)(2,1)} async-done(((bf16[384,768]{1,0:T(8,128)(2,1)}), bf16[3072,768]{1,0:T(8,128)(2,1)}) %all-gather.14.cloned.1.call-update) | async-done | bytes 4718608 | tf_op jit(solution)/shard_map/all_gather | solution.py:141
  332.9 8.2 fusion.126
  342.8 8.2 fusion.62
  360.5 134.1 %while.41 = (s32[]{:T(128)}, bf16[12,512,64]{1,2,0:T(8,128)(2,1)}, bf16[12,2048,64]{1,2,0:T(8,128)(2,1)}, bf16[12,2048,64]{1,2,0:T(8,128)(2,1)}, bf16[12,512,64]...) while((s32[]{:T(128)}, bf16[12,512,64]{1,2,0:T(8,128)(2,1)}, ...), condition=%wide.region_22.23_spmd.clone, body=%wide.region_20.22_spmd.clone.sunk | while | flops 681737728 | bytes 34628728 | solution.py:202
  494.6 6.6 pad_maximum_fusion
  501.3 56.6 %reduce-scatter.8.cloned.1.call-done = bf16[512,1536]{0,1:T(8,128)(2,1)} async-done(((bf16[2048,1536]{0,1:T(8,128)(2,1)}), bf16[512,1536]{0,1:T(8,128)(2,1)}) %reduce-scatter.8.cloned.1.call-update) | async-done | bytes 1572880 | tf_op jit(solution)/shard_map/reduce_scatter | solution.py:213
  557.8 5.7 fusion.71
  563.5 5.8 copy.56
  572.4 9.4 convolution_convert_fusion
  584.1 6.5 convolution_convert_fusion.1
  590.8 58.0 %while.39 = (s32[]{:T(128)}, bf16[12,512,64]{1,2,0:T(8,128)(2,1)S(1)}, bf16[12,512,64]{2,1,0:T(8,128)(2,1)}, bf16[12,2048,64]{2,1,0:T(8,128)(2,1)}, bf16[12,2048...) while((s32[]{:T(128)}, bf16[12,512,64]{1,2,0:T(8,128)(2,1)S(1)}, ...), condition=%wide.region_3.4_spmd.clone, body=%wide.region_0.3_spmd.clone.sunk | while | flops 277871616 | bytes 13916245 | solution.py:83
  652.1 10.1 %fusion.127 = (f32[512]{0:T(512)S(1)}, f32[512,768]{1,0:T(8,128)S(1)}) fusion(bf16[3072,768]{1,0:T(8,128)(2,1)} %all-gather.14.cloned.1.call-done, bf16[768,3072]{1,0:T(8,128)(2,1)} %all-gather.12.cloned.1.call-done, f32[512,768]{1,0:T(8,128)} %copy-done.4, f32[768]{0:T(1024)S(1)} %convert_element_type.158, f32[768]{0:T(1024)S(1)} %convert_element_type.157, ...), kind=kOutput, calls=%fused_computation.164 | convolution fusion | flops 4850318848 | bytes 12595200 | tf_op jit(solution)/shard_map/dot_general | solution.py:101
  664.7 52.1 %reduce-scatter.10.cloned.1.call-done = bf16[96,768]{1,0:T(8,128)(2,1)} async-done(((bf16[768,768]{1,0:T(8,128)(2,1)}), bf16[96,768]{1,0:T(8,128)(2,1)}) %reduce-scatter.10.cloned.1.call-update) | async-done | bytes 147472 | tf_op jit(solution)/shard_map/reduce_scatter | solution.py:223
  716.7 98.5 %reduce-scatter.14.cloned.1.call-done = bf16[384,768]{1,0:T(8,128)(2,1)} async-done(((bf16[3072,768]{1,0:T(8,128)(2,1)}), bf16[384,768]{1,0:T(8,128)(2,1)}) %reduce-scatter.14.cloned.1.call-update) | async-done | bytes 589840 | tf_op jit(solution)/shard_map/reduce_scatter | solution.py:229
  815.3 99.1 %reduce-scatter.12.cloned.1.call-done = bf16[96,3072]{1,0:T(8,128)(2,1)} async-done(((bf16[768,3072]{1,0:T(8,128)(2,1)}), bf16[96,3072]{1,0:T(8,128)(2,1)}) %reduce-scatter.12.cloned.1.call-update) | async-done | bytes 589840 | tf_op jit(solution)/shard_map/reduce_scatter | solution.py:226
  914.4 35.9 %all-reduce.8 = (bf16[768]{0:T(1024)(128)(2,1)S(1)}, bf16[768]{0:T(1024)(128)(2,1)S(1)}, bf16[768]{0:T(1024)(128)(2,1)S(1)}, bf16[768]{0:T(1024)(128)(2,1)S(1)}, bf16[768]{0:T(1024)(128)(2,1)S(1)}) all-reduce(bf16[768]{0:T(1024)(128)(2,1)S(1)} %dynamic-update-slice.3, ...), channel_id=1, replica_groups=mesh['shard'=8,'seq'=4] {'shard'}, use_global_device_ids=true, to_apply=%add.3 | all-reduce | flops 3840 | bytes 15360
  950.6 6.2 all-reduce.10
  960.0 6.0 fusion.85
  (330 shorter events, 320.1 us)
Async XLA Ops:
  7.2 70.9 %all-gather.6.cloned.1.call-start = ((), (), s32[]{:S(2)}) async-start(), calls=%async_computation.5 | async-start | bytes 3981312 | tf_op jit(solution)/shard_map/all_gather | solution.py:138
  7.9 120.9 %all-gather.8.cloned.1.call-start = ((), (), s32[]{:S(2)}) async-start(), calls=%async_computation.6 | async-start | bytes 7864320 | tf_op jit(solution)/shard_map/all_gather | solution.py:67
  82.4 3.4 copy-start.8
  82.4 4.7 copy-start.13
  82.4 4.9 copy-start.14
  82.4 5.1 copy-start.15
  82.4 24.7 %copy-start.9 = (s32[1,2048]{1,0:T(1,128)S(1)}, s32[1,2048]{1,0:T(1,128)}, u32[]{:S(2)}) copy-start(s32[1,2048]{1,0:T(1,128)} %param.18) | copy-start | bytes 24580
  83.8 168.0 %all-gather.10.cloned.1.call-start = ((), (), s32[]{:S(2)}) async-start(), calls=%async_computation.7 | async-start | bytes 1327104 | tf_op jit(solution)/shard_map/all_gather | solution.py:139
  84.5 170.3 %all-gather.12.cloned.1.call-start = ((), (), s32[]{:S(2)}) async-start(), calls=%async_computation.8 | async-start | bytes 5308416 | tf_op jit(solution)/shard_map/all_gather | solution.py:140
  85.1 247.8 %all-gather.14.cloned.1.call-start = ((), (), s32[]{:S(2)}) async-start(), calls=%async_computation.9 | async-start | bytes 5308416 | tf_op jit(solution)/shard_map/all_gather | solution.py:141
  85.7 472.2 %reduce-scatter.8.cloned.1.call-start = ((), (), s32[]{:S(2)}) async-start(), calls=%async_computation.10 | async-start | bytes 7864320 | tf_op jit(solution)/shard_map/reduce_scatter | solution.py:213
  172.9 2.0 copy-start
  189.0 2.0 copy-start
  213.6 2.0 copy-start
  221.7 2.0 copy-start
  251.8 10.1 %copy-start.2 = (bf16[12,512,64]{1,2,0:T(8,128)(2,1)}, bf16[12,512,64]{1,2,0:T(8,128)(2,1)S(1)}, u32[]{:S(2)}) copy-start(bf16[12,512,64]{1,2,0:T(8,128)(2,1)S(1)} %get-tuple-element.135) | copy-start | bytes 2359300
  261.9 79.6 %copy-start.3 = (bf16[512,768]{1,0:T(8,128)(2,1)S(1)}, bf16[512,768]{1,0:T(8,128)(2,1)}, u32[]{:S(2)}) copy-start(bf16[512,768]{1,0:T(8,128)(2,1)} %param.27) | copy-start | bytes 2359300
  332.9 9.9 %copy-start.10 = (bf16[3072,768]{1,0:T(8,128)(2,1)S(1)}, bf16[3072,768]{1,0:T(8,128)(2,1)}, u32[]{:S(2)}) copy-start(bf16[3072,768]{1,0:T(8,128)(2,1)} %all-gather.14.cloned.1.call-done) | copy-start | bytes 14155780
  332.9 9.9 %copy-start.17 = (f32[512,3072]{1,0:T(8,128)S(1)}, f32[512,3072]{1,0:T(8,128)}, u32[]{:S(2)}) copy-start(f32[512,3072]{1,0:T(8,128)} %fusion.116) | copy-start | bytes 18874372
  341.1 9.8 %copy-start.1 = (f32[512,768]{1,0:T(8,128)}, f32[512,768]{1,0:T(8,128)S(1)}, u32[]{:S(2)}) copy-start(f32[512,768]{1,0:T(8,128)S(1)} %get-tuple-element.376) | copy-start | bytes 4718596
  341.5 9.5 slice-start
  342.8 8.2 slice-start.1
  351.0 3.3 copy-start.18
  501.2 161.4 %reduce-scatter.16.cloned.1.call-start = ((), (), s32[]{:S(2)}) async-start(), calls=%async_computation.14 | async-start | bytes 3981312
  569.3 147.4 %reduce-scatter.10.cloned.1.call-start = ((), (), s32[]{:S(2)}) async-start(), calls=%async_computation.11 | async-start | bytes 1327104 | tf_op jit(solution)/shard_map/reduce_scatter | solution.py:223
  572.3 242.9 %reduce-scatter.14.cloned.1.call-start = ((), (), s32[]{:S(2)}) async-start(), calls=%async_computation.13 | async-start | bytes 5308416 | tf_op jit(solution)/shard_map/reduce_scatter | solution.py:229
  581.8 332.5 %reduce-scatter.12.cloned.1.call-start = ((), (), s32[]{:S(2)}) async-start(), calls=%async_computation.12 | async-start | bytes 5308416 | tf_op jit(solution)/shard_map/reduce_scatter | solution.py:226
  590.5 376.3 %all-reduce.14.cloned.1.call-start = ((), (), s32[]{:S(2)}) async-start(), calls=%async_computation.15 | async-start | bytes 3833856 | tf_op jit(solution)/shard_map/psum | solution.py:246
  590.8 58.0 %copy-start.12 = (bf16[512,768]{1,0:T(8,128)(2,1)S(1)}, bf16[512,768]{1,0:T(8,128)(2,1)}, u32[]{:S(2)}) copy-start(bf16[512,768]{1,0:T(8,128)(2,1)} %param.17) | copy-start | bytes 2359300
  662.2 252.1 %copy-start.7 = (bf16[768]{0:T(1024)(128)(2,1)S(1)}, bf16[768]{0:T(1024)(128)(2,1)}, u32[]{:S(2)}) copy-start(bf16[768]{0:T(1024)(128)(2,1)} %get-tuple-element.288) | copy-start | bytes 4612
  966.8 4.4 copy-start.5
  966.8 5.6 copy-start.6
  (11 other events, 19.5 us)
Sparse Core Ops, SparseCore 0:
  10.2 67.8 all-gather.5
  83.9 44.9 all-gather.7
  131.0 41.0 all-gather.9
  174.1 78.6 all-gather.11
  254.9 78.0 all-gather.13
  501.3 56.4 reduce-scatter.7
  569.4 79.1 reduce-scatter.15
  653.0 63.7 reduce-scatter.9
  720.8 94.3 reduce-scatter.13
  819.2 95.1 reduce-scatter.11
  917.7 49.0 all-reduce.13
where the time goes:
time: 992 us; the launch traced here: 980 us
  waiting for transfers between devices  471 us (47%)
  matrix products  320 us (32%)
  local copies, waits for them, and re-layouts  69.3 us (7%)
  blocking collectives  61.4 us (6%)
  other arithmetic  41.4 us (4%)
  between operations  15.9 us (2%)
    dot_general x52, matrix products, contract_cols(): lax.dot_general(left_mat, right_mat, (((1,), (1,)), ((), ())), preferred_...  116 us
    reduce_scatter x1, waiting for transfers between devices, shards(): lax.psum_scatter(grad_widen.astype(jnp.bfloat16), 'shard', scatter_dimens...  99.1 us
    reduce_scatter x1, waiting for transfers between devices, shards(): lax.psum_scatter(grad_narrow.astype(jnp.bfloat16), 'shard', scatter_dimen...  98.5 us
    dot_general x28, matrix products, contract_rows(): lax.dot_general(left_mat, right_mat, (((0,), (0,)), ((), ())), preferred_...  74.6 us
    all_gather x1, waiting for transfers between devices, shards(): lax.all_gather(down_weight, 'shard', axis=0, tiled=True)  71 us
    all_gather x1, waiting for transfers between devices, shards(): lax.all_gather(qkv_weight, 'shard', axis=0, tiled=True)  70.2 us
    dot_general x24, matrix products, one_head(): jnp.dot(attend, value_rows, preferred_element_type=jnp.float32)  65.4 us
    reduce_scatter x1, waiting for transfers between devices, shards(): lax.psum_scatter(key_part.astype(jnp.bfloat16), 'seq', scatter_dimension=...  56.6 us
  transfers between devices with their start and end apart: 11, of which 8 were waited for; matrix products, arithmetic and copies ran while one was open for 22% of the time, Pallas kernels for 0%

commit v1 on v0

v1 whole, which is shorter than its diff:
```python
from functools import partial

import jax
import jax.numpy as jnp
from jax import lax
from jax.experimental import pallas as pl
from jax.experimental.pallas import tpu as pltpu
from jax.sharding import PartitionSpec as P

HEADS = 12
HEAD_DIM = 64
GROUPS = 16
EPSILON = 1e-12
FAR = -(2.0**30)
SCALE = HEAD_DIM**-0.5
BQ = 256
BK = 256
BF = jnp.bfloat16
F32 = jnp.float32


def dot(a, b, ca, cb):
    return lax.dot_general(a, b, (((ca,), (cb,)), ((), ())), preferred_element_type=F32)


def doc_rows(ids_ref, same, other):
    ids = ids_ref[...]
    rows = lax.broadcasted_iota(jnp.int32, (GROUPS, ids.shape[1]), 0)
    return jnp.where(rows == ids, same, other).astype(BF)


def fill_tokens(info, own, recv, ids_ref, nq, q_t, k_nat, v_t, k_t, v_nat):
    half = own.shape[1]
    total = 2 * half
    place = info[2 * nq]
    q_t[HEAD_DIM : HEAD_DIM + GROUPS, :] = doc_rows(ids_ref, 0.0, FAR)
    q_t[HEAD_DIM + GROUPS :, :] = jnp.zeros((128 - HEAD_DIM - GROUPS, total), BF)
    for side, ref in ((place, own), (1 - place, recv)):
        at = pl.multiple_of(side * half, half)
        q_t[:HEAD_DIM, pl.ds(at, half)] = ref[:HEAD_DIM, :] * SCALE
        keys = ref[HEAD_DIM : 2 * HEAD_DIM, :]
        values = ref[2 * HEAD_DIM :, :]
        if k_t is not None:
            k_t[:, pl.ds(at, half)] = keys
        if v_t is not None:
            v_t[:, pl.ds(at, half)] = values
        k_nat[pl.ds(at, half), :HEAD_DIM] = keys.T
        if v_nat is not None:
            v_nat[pl.ds(at, half), :] = jnp.concatenate(
                [values, jnp.zeros((128 - HEAD_DIM, half), BF)], 0
            ).T
    docs = jnp.concatenate(
        [doc_rows(ids_ref, 1.0, 0.0), jnp.zeros((128 - HEAD_DIM - GROUPS, total), BF)], 0
    )
    k_nat[:, HEAD_DIM:] = docs.T


def attend_kernel(nq, info, own, recv, ids_ref, ctx_own, ctx_send, ctx_full, lse, q_t, k_nat, v_t):
    half = own.shape[1]
    fill_tokens(info, own, recv, ids_ref, nq, q_t, k_nat, v_t, None, None)

    def query_block(i, carry):
        at = pl.multiple_of(i * BQ, BQ)
        query = q_t[:, pl.ds(at, BQ)]

        def key_block(k, state):
            top, total, acc = state
            kat = pl.multiple_of(k * BK, BK)
            scores = jnp.dot(k_nat[pl.ds(kat, BK), :], query, preferred_element_type=F32)
            new_top = jnp.maximum(top, jnp.max(scores, 0, keepdims=True))
            powers = jnp.exp(scores - new_top)
            fade = jnp.exp(top - new_top)
            total = total * fade + jnp.sum(powers, 0, keepdims=True)
            acc = acc * fade + jnp.dot(
                v_t[:, pl.ds(kat, BK)], powers.astype(BF), preferred_element_type=F32
            )
            return new_top, total, acc

        top, total, acc = lax.fori_loop(
            info[i],
            info[nq + i],
            key_block,
            (
                jnp.full((1, BQ), -3e38, F32),
                jnp.zeros((1, BQ), F32),
                jnp.zeros((HEAD_DIM, BQ), F32),
            ),
        )
        ctx_full[:, pl.ds(at, BQ)] = acc / total
        lse[:, pl.ds(at, BQ)] = top + jnp.log(total)
        return carry

    lax.fori_loop(0, nq, query_block, 0)
    place = info[2 * nq]
    ctx_own[...] = ctx_full[:, pl.ds(pl.multiple_of(place * half, half), half)].astype(BF)
    ctx_send[...] = ctx_full[:, pl.ds(pl.multiple_of((1 - place) * half, half), half)].astype(BF)


def attend(info, own, recv, ids):
    half = own.shape[1]
    total = 2 * half
    nq = total // BQ
    vm = pl.BlockSpec(memory_space=pltpu.VMEM)
    return pl.pallas_call(
        partial(attend_kernel, nq),
        out_shape=(
            jax.ShapeDtypeStruct((HEAD_DIM, half), BF),
            jax.ShapeDtypeStruct((HEAD_DIM, half), BF),
            jax.ShapeDtypeStruct((HEAD_DIM, total), F32),
            jax.ShapeDtypeStruct((1, total), F32),
        ),
        in_specs=[pl.BlockSpec(memory_space=pltpu.SMEM), vm, vm, vm],
        out_specs=(vm, vm, vm, vm),
        scratch_shapes=[
            pltpu.VMEM((128, total), BF),
            pltpu.VMEM((total, 128), BF),
            pltpu.VMEM((HEAD_DIM, total), BF),
        ],
        cost_estimate=pl.CostEstimate(
            flops=4 * total * total * HEAD_DIM, bytes_accessed=8 * 192 * total, transcendentals=total * total // 3
        ),
        name="attend",
    )(info, own, recv, ids)


def attend_back_kernel(
    nq, info, own, recv, g_own, g_recv, ids_ref, ctx_full, lse, out_own, out_send,
    q_t, k_nat, k_t, v_nat, g_t, qg_nat, acc, dq_t,
):
    half = own.shape[1]
    place = info[2 * nq]
    fill_tokens(info, own, recv, ids_ref, nq, q_t, k_nat, None, k_t, v_nat)
    g_t[HEAD_DIM:, :] = jnp.zeros((128 - HEAD_DIM, 2 * half), BF)
    for side, ref, grad in ((place, own, g_own), (1 - place, recv, g_recv)):
        at = pl.multiple_of(side * half, half)
        g_t[:HEAD_DIM, pl.ds(at, half)] = grad[...]
        qg_nat[pl.ds(at, half), :] = jnp.concatenate([ref[:HEAD_DIM, :] * SCALE, grad[...]], 0).T
    acc[...] = jnp.zeros_like(acc)

    def query_block(i, carry):
        at = pl.multiple_of(i * BQ, BQ)
        query = q_t[:, pl.ds(at, BQ)]
        grad = g_t[:, pl.ds(at, BQ)]
        row_term = jnp.sum(
            ctx_full[:, pl.ds(at, BQ)] * grad[:HEAD_DIM].astype(F32), 0, keepdims=True
        )
        log_total = lse[:, pl.ds(at, BQ)]
        natural = qg_nat[pl.ds(at, BQ), :]
        left = lax.broadcasted_iota(jnp.int32, (BK, 128), 1) < HEAD_DIM

        def key_block(k, dq):
            kat = pl.multiple_of(k * BK, BK)
            scores = jnp.dot(k_nat[pl.ds(kat, BK), :], query, preferred_element_type=F32)
            chance = jnp.exp(scores - log_total)
            grad_chance = jnp.dot(v_nat[pl.ds(kat, BK), :], grad, preferred_element_type=F32)
            grad_scores = (chance * (grad_chance - row_term)).astype(BF)
            dq = dq + jnp.dot(k_t[:, pl.ds(kat, BK)], grad_scores, preferred_element_type=F32)
            acc[pl.ds(kat, BK), :] += jnp.where(
                left,
                jnp.dot(grad_scores, natural, preferred_element_type=F32),
                jnp.dot(chance.astype(BF), natural, preferred_element_type=F32),
            )
            return dq

        dq_t[:, pl.ds(at, BQ)] = (
            lax.fori_loop(info[i], info[nq + i], key_block, jnp.zeros((HEAD_DIM, BQ), F32)) * SCALE
        )
        return carry

    lax.fori_loop(0, nq, query_block, 0)
    for side, out in ((place, out_own), (1 - place, out_send)):
        at = pl.multiple_of(side * half, half)
        out[:HEAD_DIM, :] = dq_t[:, pl.ds(at, half)].astype(BF)
        out[HEAD_DIM:, :] = acc[pl.ds(at, half), :].T.astype(BF)


def attend_back(info, own, recv, g_own, g_recv, ids, ctx_full, lse):
    half = own.shape[1]
    total = 2 * half
    nq = total // BQ
    vm = pl.BlockSpec(memory_space=pltpu.VMEM)
    return pl.pallas_call(
        partial(attend_back_kernel, nq),
        out_shape=(
            jax.ShapeDtypeStruct((3 * HEAD_DIM, half), BF),
            jax.ShapeDtypeStruct((3 * HEAD_DIM, half), BF),
        ),
        in_specs=[pl.BlockSpec(memory_space=pltpu.SMEM)] + [vm] * 7,
        out_specs=(vm, vm),
        scratch_shapes=[
            pltpu.VMEM((128, total), BF),
            pltpu.VMEM((total, 128), BF),
            pltpu.VMEM((HEAD_DIM, total), BF),
            pltpu.VMEM((total, 128), BF),
            pltpu.VMEM((128, total), BF),
            pltpu.VMEM((total, 128), BF),
            pltpu.VMEM((total, 128), F32),
            pltpu.VMEM((HEAD_DIM, total), F32),
        ],
        cost_estimate=pl.CostEstimate(
            flops=10 * total * total * HEAD_DIM, bytes_accessed=12 * 192 * total, transcendentals=total * total // 3
        ),
        name="attend_back",
    )(info, own, recv, g_own, g_recv, ids, ctx_full, lse)


def norm_rows(hidden, gain_vec, shift_vec):
    row_mean = jnp.mean(hidden, -1, keepdims=True)
    centred = hidden - row_mean
    variance = jnp.mean(centred * centred, -1, keepdims=True)
    inverse = lax.rsqrt(variance + EPSILON)
    normed = centred * inverse
    return (normed * gain_vec + shift_vec, normed, inverse)


def norm_back(grad_y, normed, inverse, gain_vec):
    grad_n = grad_y * gain_vec
    bracket = (
        grad_n
        - jnp.mean(grad_n, -1, keepdims=True)
        - normed * jnp.mean(grad_n * normed, -1, keepdims=True)
    )
    return (inverse * bracket, jnp.sum(grad_y * normed, 0), jnp.sum(grad_y, 0))


def gelu_both(u):
    root = 0.7978845608028654
    t = jnp.tanh(root * (u + 0.044715 * (u * u * u)))
    act = 0.5 * u * (1.0 + t)
    slope = 0.5 * (1.0 + t) + 0.5 * u * (1.0 - t * t) * (root * (1.0 + 3 * 0.044715 * (u * u)))
    return act, slope


def shards(
    n_shard,
    tokens,
    segment_ids,
    qkv_weight,
    out_weight,
    up_weight,
    down_weight,
    first_gain,
    first_bias,
    second_gain,
    second_bias,
    out_grad,
):
    rows, width = tokens.shape
    shard = lax.axis_index("shard")
    seq = lax.axis_index("seq")
    xb, cb = seq // 2, seq % 2
    bits = [1 << b for b in range(n_shard.bit_length() - 1)]
    top = bits[-1]
    owner = (shard // top) % 2 == cb

    def swap(value, mask):
        return lax.ppermute(value, "shard", [(i, i ^ mask) for i in range(n_shard)])

    def swap_core(value):
        return lax.ppermute(value, "seq", [(i, i ^ 1) for i in range(4)])

    def swap_x(value):
        return lax.ppermute(value, "seq", [(i, i ^ 2) for i in range(4)])

    def to_core(value, to_owner):
        pairs = []
        for sh in range(n_shard):
            for se in range(4):
                if (sh // top == se % 2) != to_owner:
                    pairs.append((sh * 4 + se, (sh ^ top) * 4 + se))
        return lax.ppermute(value, ("shard", "seq"), pairs)

    def ordered(flag, own, other, axis):
        return jnp.where(
            flag == 0, jnp.stack([own, other], axis), jnp.stack([other, own], axis)
        )

    def gather(block, over):
        value = block[None]
        for bit in over:
            value = ordered((shard // bit) % 2, value, swap(value, bit), 1)
            value = value.reshape((-1,) + block.shape)
        return value.reshape((-1,) + block.shape[1:])

    def gather_half(block):
        there = to_core(block, False)
        return gather(jnp.where(owner, block, there), bits[-2::-1])

    def reduce(partial_sum, over, blocks):
        value = partial_sum.reshape((blocks, -1) + partial_sum.shape[1:])
        for bit in over:
            pairs = value.reshape((value.shape[0] // 2, 2) + value.shape[1:])
            flag = (shard // bit) % 2
            mine = jnp.where(flag == 0, pairs[:, 0], pairs[:, 1])
            theirs = jnp.where(flag == 0, pairs[:, 1], pairs[:, 0])
            value = (mine.astype(F32) + swap(theirs, bit).astype(F32)).astype(BF)
        return value[0]

    def add_x(value):
        return (value.astype(F32) + swap_x(value).astype(F32)).astype(BF)

    def reduce_cols(partial_sum):
        return add_x(reduce(partial_sum, bits, n_shard))

    def reduce_half(partial_sum):
        value = reduce(partial_sum, bits[:-1], n_shard // 2)
        there = to_core(value, True)
        value = add_x((value.astype(F32) + there.astype(F32)).astype(BF))
        return jnp.where(owner, value, swap_core(value))

    def pick(value, flag, axis):
        return jnp.where(flag == 0, lax.index_in_dim(value, 0, axis, False), lax.index_in_dim(value, 1, axis, False))

    def chip_rows(value):
        both = ordered(cb, value, swap_core(value), 0)
        return both.reshape((2 * rows,) + value.shape[1:])

    def core_sum(partial_sum):
        halves = partial_sum.reshape(2, rows, -1)
        return pick(halves, cb, 0) + swap_core(pick(halves, 1 - cb, 0).astype(BF)).astype(F32)

    half_width = width // 2
    chip_tokens = chip_rows(tokens)
    sections = lax.dynamic_slice_in_dim(
        qkv_weight.reshape(-1, 3, width), cb * half_width, half_width, 2
    )
    qkv_parts = [
        gather(sections[:, :, j * 128 : (j + 1) * 128].reshape(-1, 384), bits[::-1]) for j in range(3)
    ]
    vectors = jnp.stack([first_gain, first_bias, second_gain, second_bias])
    vectors = jnp.concatenate([vectors, vectors, vectors, vectors], 0)
    vectors = gather(vectors[None], bits[::-1])[:, :4].transpose(1, 0, 2).reshape(4, width).astype(F32)
    gain_one, bias_one, gain_two, bias_two = vectors[0], vectors[1], vectors[2], vectors[3]
    mixer = gather_half(out_weight)
    ff_half = up_weight.shape[1] // 2
    widen = gather(lax.dynamic_slice_in_dim(up_weight, cb * ff_half, ff_half, 1), bits[::-1])
    narrow = gather_half(down_weight)

    ids = segment_ids[0]
    length = ids.shape[0]
    nq = length // BQ
    first = ids.reshape(nq, BQ)[:, 0]
    last = ids.reshape(nq, BQ)[:, -1]
    begin = jnp.sum((ids[None] < first[:, None]).astype(jnp.int32), 1) // BK
    end = (jnp.sum((ids[None] <= last[:, None]).astype(jnp.int32), 1) + BK - 1) // BK
    info = jnp.concatenate([begin, end, xb[None].astype(jnp.int32)])
    ids_row = ids[None]
    saved = []
    context = []
    for j in range(3):
        merged = dot(qkv_parts[j], chip_tokens, 0, 1).astype(BF).reshape(3, 2, HEAD_DIM, 2 * rows)
        own = pick(merged, xb, 1).reshape(3 * HEAD_DIM, 2 * rows)
        recv = swap_x(pick(merged, 1 - xb, 1).reshape(3 * HEAD_DIM, 2 * rows))
        ctx_own, ctx_send, ctx_full, lse = attend(info, own, recv, ids_row)
        context.append(ordered(xb, ctx_own, swap_x(ctx_send), 0))
        saved.append((own, recv, ctx_full, lse))
    context = jnp.stack(context).reshape(half_width, 2 * rows)

    attn_out = core_sum(dot(context, mixer, 0, 0))
    first_norm, normed_one, inverse_one = norm_rows(
        tokens.astype(F32) + attn_out, gain_one, bias_one
    )
    first_low = chip_rows(first_norm.astype(BF))
    act, slope = gelu_both(dot(first_low, widen, 1, 0))
    act_low = act.astype(BF)
    slope_low = slope.astype(BF)
    mlp_out = core_sum(dot(act_low, narrow, 1, 0))
    result, normed_two, inverse_two = norm_rows(first_norm + mlp_out, gain_two, bias_two)

    grad_two, late_gain, late_shift = norm_back(
        out_grad.astype(F32), normed_two, inverse_two, gain_two
    )
    grad_mlp = chip_rows(grad_two.astype(BF))
    grad_pre = (dot(grad_mlp, narrow, 1, 1) * slope_low.astype(F32)).astype(BF)
    grad_first = grad_two + core_sum(dot(grad_pre, widen, 1, 1))
    grad_one, early_gain, early_shift = norm_back(grad_first, normed_one, inverse_one, gain_one)
    grad_attn = chip_rows(grad_one.astype(BF))
    grad_context = dot(mixer, grad_attn, 1, 1).astype(BF).reshape(3, 2, HEAD_DIM, 2 * rows)
    g_own = pick(grad_context, xb, 1)
    g_recv = swap_x(pick(grad_context, 1 - xb, 1))

    narrow_grad = reduce_half(dot(act_low, grad_mlp, 0, 0).astype(BF))
    widen_grad = reduce_cols(dot(first_low, grad_pre, 0, 0).astype(BF))
    mixer_grad = reduce_half(dot(context, grad_attn, 1, 0).astype(BF))

    sums = jnp.stack([early_gain, early_shift, late_gain, late_shift])
    sums = sums + swap_core(sums)
    sums = sums.reshape(4, n_shard, -1).transpose(1, 0, 2)
    sums = jnp.concatenate([sums, jnp.zeros_like(sums), jnp.zeros_like(sums), jnp.zeros_like(sums)], 1).astype(BF)
    sums = add_x(reduce(sums.reshape(n_shard * 16, -1), bits, n_shard)).astype(F32)

    grads = []
    qkv_grads = []
    for j in range(3):
        own, recv, ctx_full, lse = saved[j]
        d_own, d_send = attend_back(
            info, own, recv, g_own[j], g_recv[j], ids_row, ctx_full, lse
        )
        d_recv = swap_x(d_send)
        both = ordered(
            xb, d_own.reshape(3, HEAD_DIM, -1), d_recv.reshape(3, HEAD_DIM, -1), 1
        ).reshape(384, 2 * rows)
        grads.append(both)
        qkv_grads.append(reduce_cols(dot(chip_tokens, both, 0, 1).astype(BF)))
    back = sum(dot(grads[j], qkv_parts[j], 0, 1) for j in range(3))
    input_grad = grad_one + core_sum(back)

    mine = jnp.concatenate([g.reshape(-1, 3, 128) for g in qkv_grads], 2)
    qkv_grad = ordered(cb, mine, swap_core(mine), 2).reshape(mine.shape[0], 3 * width)
    widen_grad = ordered(cb, widen_grad, swap_core(widen_grad), 1).reshape(-1, 2 * ff_half)
    return (
        result.astype(BF),
        input_grad,
        qkv_grad.astype(F32),
        mixer_grad.astype(F32),
        widen_grad.astype(F32),
        narrow_grad.astype(F32),
        sums[0],
        sums[1],
        sums[2],
        sums[3],
    )


def solution(mesh):
    placed = (
        P(("shard", "seq"), None),
        P("shard", None),
        P("shard", None),
        P("shard", None),
        P("shard", None),
        P("shard", None),
        P("shard"),
        P("shard"),
        P("shard"),
        P("shard"),
        P(("shard", "seq"), None),
    )
    return jax.shard_map(
        partial(shards, mesh.shape["shard"]),
        mesh=mesh,
        in_specs=placed,
        out_specs=(
            P(("shard", "seq"), None),
            P(("shard", "seq"), None),
            P("shard", None),
            P("shard", None),
            P("shard", None),
            P("shard", None),
            P("shard"),
            P("shard"),
            P("shard"),
            P("shard"),
        ),
        check_vma=False,
    )
```

time: 992 us -> 492 us (0.50)
  matrix products: 320 us -> 35.2 us
  waiting for transfers between devices: 471 us -> 192 us
  Pallas kernels: 0 us -> 109 us
  starting transfers between devices: 0.61 us -> 81.8 us
  blocking collectives: 61.4 us -> 0 us
  local copies, waits for them, and re-layouts: 69.3 us -> 18.5 us
  between operations: 15.9 us -> 2.66 us
    reduce_scatter x4 -> x0, waiting for transfers between devices: 306 us -> none  [the longest x1 99.1 us: shards(): lax.psum_scatter(grad_widen.astype(jnp.bfloat16), 'shard', scatter_dimens...]
    dot_general x122 -> x18, matrix products: 320 us -> 35.2 us  [dot(): lax.dot_general(a, b, (((ca,), (cb,)), ((), ())), preferred_element_type=...]
    ppermute x0 -> x72, waiting for transfers between devices: none -> 192 us  [the longest x38 155 us: swap(): return lax.ppermute(value, 'shard', [(i, i ^ mask) for i in range(n_shard)])]
    all_gather x5 -> x0, waiting for transfers between devices: 161 us -> none  [the longest x1 71 us: shards(): lax.all_gather(down_weight, 'shard', axis=0, tiled=True)]
    pallas_call x0 -> x6, Pallas kernels: none -> 109 us  [the longest x3 56.6 us: attend_back(): pl.pallas_call(partial(attend_back_kernel, nq), out_shape=(jax.ShapeDtype...]
    ppermute x0 -> x72, starting transfers between devices: none -> 81.8 us  [the longest x38 52.8 us: swap(): return lax.ppermute(value, 'shard', [(i, i ^ mask) for i in range(n_shard)])]
    unnamed x2 -> x0, blocking collectives: 55.2 us -> none
    while x24 -> x0, local copies, waits for them, and re-layouts: 23.5 us -> none
  transfers between devices with their start and end apart: 11 -> 72, of which waited for: 8 -> 32; matrix products, arithmetic and copies ran while one was open for 22% -> 12% of each run, Pallas kernels for 0% -> 23%
where the time goes in v1:
time: 492 us; the launch traced here: 485 us
  waiting for transfers between devices  192 us (39%)
  Pallas kernels  109 us (22%)
  starting transfers between devices  81.8 us (17%)
  other arithmetic  45.1 us (9%)
  matrix products  35.2 us (7%)
  local copies, waits for them, and re-layouts  18.5 us (4%)
    ppermute x38, waiting for transfers between devices, swap(): return lax.ppermute(value, 'shard', [(i, i ^ mask) for i in range(n_shard)])  155 us
    pallas_call x3, Pallas kernels, attend_back(): pl.pallas_call(partial(attend_back_kernel, nq), out_shape=(jax.ShapeDtype...  56.6 us
    ppermute x38, starting transfers between devices, swap(): return lax.ppermute(value, 'shard', [(i, i ^ mask) for i in range(n_shard)])  52.8 us
    pallas_call x3, Pallas kernels, attend(): pl.pallas_call(partial(attend_kernel, nq), out_shape=(jax.ShapeDtypeStruc...  52.6 us
    dot_general x18, matrix products, dot(): lax.dot_general(a, b, (((ca,), (cb,)), ((), ())), preferred_element_type=...  35.2 us
    ppermute x17, waiting for transfers between devices, swap_x(): return lax.ppermute(value, 'seq', [(i, i ^ 2) for i in range(4)])  31.4 us
    ppermute x17, starting transfers between devices, swap_x(): return lax.ppermute(value, 'seq', [(i, i ^ 2) for i in range(4)])  19.3 us
    select_n x36, other arithmetic, ordered(): jnp.where(flag == 0, jnp.stack([own, other], axis), jnp.stack([other, own...  11.1 us
  transfers between devices with their start and end apart: 72, of which 32 were waited for; matrix products, arithmetic and copies ran while one was open for 12% of the time, Pallas kernels for 23%

profile of v1, /device:TPU:0, one launch (start us, length us, event | category | flops | bytes accessed | tf_op | source)
XLA Modules:
  0.0 484.9 jit_solution(1896503841213884412)
XLA Ops:
  2.2 4.1 collective-permute-start.20
  24.4 3.8 collective-permute-start
  28.4 4.8 collective-permute-done.11
  36.4 3.8 collective-permute-start.7
  40.4 10.8 %collective-permute-done.7 = bf16[2,96,384]{2,1,0:T(8,128)(2,1)S(1)} collective-permute-done((bf16[2,96,384]{2,1,0:T(8,128)(2,1)S(1)}, bf16[2,96,384]{2,1,0:T(8,128)(2,1)S(1)}, u32[]{:S(2)}, u32[]{:S(2)}) %collective-permute-start.7) | collective-permute-done | bytes 147488 | tf_op jit(solution)/shard_map/ppermute | solution.py:257
  54.5 3.5 collective-permute-done.1
  62.8 5.0 %collective-permute-done.13 = bf16[4,96,384]{2,1,0:T(8,128)(2,1)S(1)} collective-permute-done((bf16[4,96,384]{2,1,0:T(8,128)(2,1)S(1)}, bf16[4,96,384]{2,1,0:T(8,128)(2,1)S(1)}, u32[]{:S(2)}, u32[]{:S(2)}) %collective-permute-start.13) | collective-permute-done | bytes 294944 | tf_op jit(solution)/shard_map/ppermute | solution.py:257
  69.8 4.4 collective-permute-done.8
  74.4 6.1 %collective-permute-done.2 = bf16[4,96,384]{2,1,0:T(8,128)(2,1)S(1)} collective-permute-done((bf16[4,96,384]{2,1,0:T(8,128)(2,1)S(1)}, bf16[4,96,384]{2,1,0:T(8,128)(2,1)S(1)}, u32[]{:S(2)}, u32[]{:S(2)}) %collective-permute-start.2) | collective-permute-done | bytes 294944 | tf_op jit(solution)/shard_map/ppermute | solution.py:257
  90.2 16.4 %collective-permute-done.4.recv = bf16[192,1024]{1,0:T(8,128)(2,1)S(1)} collective-permute-done((bf16[192,1024]{1,0:T(8,128)(2,1)S(1)}, bf16[192,1024]{1,0:T(8,128)(2,1)S(1)}, u32[]{:S(2)}, u32[]{:S(2)}) %collective-permute-start.4) | collective-permute-done | bytes 393248 | tf_op jit(solution)/shard_map/ppermute | solution.py:263
  107.4 17.4 %attend.3 = (bf16[64,1024]{1,0:T(8,128)(2,1)}, bf16[64,1024]{1,0:T(8,128)(2,1)}, f32[64,2048]{1,0:T(8,128)}, f32[1,2048]{1,0:T(1,128)}) custom-call(s32[17]{0:T(128)} %pad_add_fusion.info, bf16[192,1024]{1,0:T(8,128)(2,1)} %bitcast.603, bf16[192,1024]{1,0:T(8,128)(2,1)} %copy-done.35, s32[1,2048]{1,0:T(1,128)} %ids_ref.11), custom_call_target="tpu_custom_call" | custom-call | flops 1073741824 | bytes 3145728 | tf_op jit(solution)/shard_map/attend/pallas_call | solution.py:104
  126.5 17.4 %attend.4 = (bf16[64,1024]{1,0:T(8,128)(2,1)}, bf16[64,1024]{1,0:T(8,128)(2,1)}, f32[64,2048]{1,0:T(8,128)}, f32[1,2048]{1,0:T(1,128)}) custom-call(s32[17]{0:T(128)} %pad_add_fusion.info, bf16[192,1024]{1,0:T(8,128)(2,1)} %bitcast.607, bf16[192,1024]{1,0:T(8,128)(2,1)} %collective-permute-done.9.recv, s32[1,2048]{1,0:T(1,128)} %ids_ref.11), custom_call_target="tpu_custom_call" | custom-call | flops 1073741824 | bytes 3145728 | tf_op jit(solution)/shard_map/attend/pallas_call | solution.py:104
  144.2 17.8 %attend.5 = (bf16[64,1024]{1,0:T(8,128)(2,1)}, bf16[64,1024]{1,0:T(8,128)(2,1)}, f32[64,2048]{1,0:T(8,128)}, f32[1,2048]{1,0:T(1,128)}) custom-call(s32[17]{0:T(128)} %pad_add_fusion.info, bf16[192,1024]{1,0:T(8,128)(2,1)} %bitcast.605, bf16[192,1024]{1,0:T(8,128)(2,1)} %collective-permute-done.14.recv, s32[1,2048]{1,0:T(1,128)} %ids_ref.11), custom_call_target="tpu_custom_call" | custom-call | flops 1073741824 | bytes 3145728 | tf_op jit(solution)/shard_map/attend/pallas_call | solution.py:104
  176.5 25.2 %collective-permute-done.26 = bf16[4,96,1536]{2,1,0:T(8,128)(2,1)S(1)} collective-permute-done((bf16[4,96,1536]{2,1,0:T(8,128)(2,1)S(1)}, bf16[4,96,1536]{2,1,0:T(8,128)(2,1)S(1)}, u32[]{:S(2)}, u32[]{:S(2)}) %collective-permute-start.26) | collective-permute-done | bytes 1179680 | tf_op jit(solution)/shard_map/ppermute | solution.py:257
  202.4 23.4 %collective-permute-done.29 = bf16[2,384,768]{2,1,0:T(8,128)(2,1)S(1)} collective-permute-done((bf16[2,384,768]{2,1,0:T(8,128)(2,1)S(1)}, bf16[2,384,768]{2,1,0:T(8,128)(2,1)S(1)}, u32[]{:S(2)}, u32[]{:S(2)}) %collective-permute-start.29) | collective-permute-done | bytes 1179680 | tf_op jit(solution)/shard_map/ppermute | solution.py:257
  229.1 3.7 fusion.64
  248.6 7.3 %multiply_convert_fusion = bf16[1024,1536]{1,0:T(8,128)(2,1)S(1)} fusion(bf16[1024,768]{1,0:T(8,128)(2,1)S(1)} %bitcast.578, bf16[1536,768]{1,0:T(8,128)(2,1)S(1)} %bitcast.559, f32[1024,1536]{1,0:T(8,128)} %copy-done.36), kind=kOutput, calls=%fused_computation.11 | convolution fusion | flops 2447376384 | bytes 13369344 | tf_op jit(solution)/shard_map/dot_general | solution.py:23
  261.9 4.8 convolution_convert_fusion
  275.5 3.6 collective-permute-done.69
  280.1 3.6 collective-permute-done.70
  287.9 14.3 %collective-permute-done.62 = bf16[2,384,768]{2,1,0:T(8,128)(2,1)S(1)} collective-permute-done((bf16[2,384,768]{2,1,0:T(8,128)(2,1)S(1)}, bf16[2,384,768]{2,1,0:T(8,128)(2,1)S(1)}, u32[]{:S(2)}, u32[]{:S(2)}) %collective-permute-start.62) | collective-permute-done | bytes 1179680 | tf_op jit(solution)/shard_map/ppermute | solution.py:257
  302.8 23.8 %collective-permute-done.57 = bf16[4,96,1536]{2,1,0:T(8,128)(2,1)S(1)} collective-permute-done((bf16[4,96,1536]{2,1,0:T(8,128)(2,1)S(1)}, bf16[4,96,1536]{2,1,0:T(8,128)(2,1)S(1)}, u32[]{:S(2)}, u32[]{:S(2)}) %collective-permute-start.57) | collective-permute-done | bytes 1179680 | tf_op jit(solution)/shard_map/ppermute | solution.py:257
  336.9 4.8 collective-permute-done.58
  341.9 3.6 collective-permute-start.59
  349.0 18.8 %attend_back.4 = (bf16[192,1024]{1,0:T(8,128)(2,1)}, bf16[192,1024]{1,0:T(8,128)(2,1)}) custom-call(s32[17]{0:T(128)} %pad_add_fusion.info, bf16[192,1024]{1,0:T(8,128)(2,1)} %bitcast.608, bf16[192,1024]{1,0:T(8,128)(2,1)} %collective-permute-done.9.recv, bf16[64,1024]{1,0:T(8,128)(2,1)} %get-tuple-element.87.g_own, ...), custom_call_target="tpu_custom_call" | custom-call | flops 2684354560 | bytes 4718592 | tf_op jit(solution)/shard_map/attend_back/pallas_call | solution.py:182
  370.5 18.8 %attend_back.5 = (bf16[192,1024]{1,0:T(8,128)(2,1)}, bf16[192,1024]{1,0:T(8,128)(2,1)}) custom-call(s32[17]{0:T(128)} %pad_add_fusion.info, bf16[192,1024]{1,0:T(8,128)(2,1)} %bitcast.606, bf16[192,1024]{1,0:T(8,128)(2,1)} %collective-permute-done.14.recv, bf16[64,1024]{1,0:T(8,128)(2,1)} %get-tuple-element.86.g_own, ...), custom_call_target="tpu_custom_call" | custom-call | flops 2684354560 | bytes 4718592 | tf_op jit(solution)/shard_map/attend_back/pallas_call | solution.py:182
  390.7 19.0 %attend_back.3 = (bf16[192,1024]{1,0:T(8,128)(2,1)}, bf16[192,1024]{1,0:T(8,128)(2,1)}) custom-call(s32[17]{0:T(128)} %pad_add_fusion.info, bf16[192,1024]{1,0:T(8,128)(2,1)} %bitcast.604, bf16[192,1024]{1,0:T(8,128)(2,1)} %copy-done.35, bf16[64,1024]{1,0:T(8,128)(2,1)} %get-tuple-element.88.g_own, bf16[64,1024]{1,0:T(8,128)(2,1)} %get-tuple-element.85.g_recv, ...), custom_call_target="tpu_custom_call" | custom-call | flops 2684354560 | bytes 4718592 | tf_op jit(solution)/shard_map/attend_back/pallas_call | solution.py:182
  412.0 10.4 %collective-permute-done.55 = bf16[96,768]{1,0:T(8,128)(2,1)S(1)} collective-permute-done((bf16[96,768]{1,0:T(8,128)(2,1)S(1)}, bf16[96,768]{1,0:T(8,128)(2,1)S(1)}, u32[]{:S(2)}, u32[]{:S(2)}) %collective-permute-start.55) | collective-permute-done | bytes 147488 | tf_op jit(solution)/shard_map/ppermute | solution.py:263
  439.1 5.1 %collective-permute-done.43 = bf16[4,96,384]{2,1,0:T(8,128)(2,1)S(1)} collective-permute-done((bf16[4,96,384]{2,1,0:T(8,128)(2,1)S(1)}, bf16[4,96,384]{2,1,0:T(8,128)(2,1)S(1)}, u32[]{:S(2)}, u32[]{:S(2)}) %collective-permute-start.43) | collective-permute-done | bytes 294944 | tf_op jit(solution)/shard_map/ppermute | solution.py:257
  444.3 5.7 %collective-permute-done.47 = bf16[4,96,384]{2,1,0:T(8,128)(2,1)S(1)} collective-permute-done((bf16[4,96,384]{2,1,0:T(8,128)(2,1)S(1)}, bf16[4,96,384]{2,1,0:T(8,128)(2,1)S(1)}, u32[]{:S(2)}, u32[]{:S(2)}) %collective-permute-start.47) | collective-permute-done | bytes 294944 | tf_op jit(solution)/shard_map/ppermute | solution.py:257
  453.6 3.7 collective-permute-start.41
  463.9 3.7 collective-permute-done.45
  (391 shorter events, 163.6 us)
Async XLA Ops:
  6.3 34.0 %collective-permute-start.16 = (bf16[96,768]{1,0:T(8,128)(2,1)}, bf16[96,768]{1,0:T(8,128)(2,1)}, u32[]{:S(2)}, u32[]{:S(2)}) collective-permute-start(bf16[96,768]{1,0:T(8,128)(2,1)} %param.14), channel_id=1, source_target_pairs={{0,16},{2,18},{4,20},{6,22},{8,24},{10,26},{12,28},{14,30},{17,1},... | collective-permute-start | bytes 442376 | tf_op jit(solution)/shard_map/ppermute | solution.py:271
  9.9 49.8 %collective-permute-start.24 = (bf16[1,96,1536]{2,1,0:T(8,128)(2,1)S(1)}, bf16[1,96,1536]{2,1,0:T(8,128)(2,1)S(1)}, u32[]{:S(2)}, u32[]{:S(2)}) collective-permute-start(bf16[1,96,1536]{2,1,0:T(8,128)(2,1)S(1)} %get-tuple-element.79), channel_id=1, source_target_pairs={{0,16},{4,20},{8,24},{12,28},{16,0},{20,4},{24,8},{28,12},{1,17},{... | collective-permute-start | bytes 884744 | tf_op jit(solution)/shard_map/ppermute | solution.py:257
  11.9 21.3 %collective-permute-start.11 = (bf16[1,96,384]{2,1,0:T(8,128)(2,1)S(1)}, bf16[1,96,384]{2,1,0:T(8,128)(2,1)S(1)}, u32[]{:S(2)}, u32[]{:S(2)}) collective-permute-start(bf16[1,96,384]{2,1,0:T(8,128)(2,1)S(1)} %broadcast_in_dim_reshape.11), channel_id=1, source_target_pairs={{0,16},{4,20},{8,24},{12,28},{16,0},{20,4},{24,8},{28,12},{1,17},{... | collective-permute-start | bytes 221192 | tf_op jit(solution)/shard_map/ppermute | solution.py:257
  14.9 19.8 %collective-permute-start.6 = (bf16[1,96,384]{2,1,0:T(8,128)(2,1)S(1)}, bf16[1,96,384]{2,1,0:T(8,128)(2,1)S(1)}, u32[]{:S(2)}, u32[]{:S(2)}) collective-permute-start(bf16[1,96,384]{2,1,0:T(8,128)(2,1)S(1)} %broadcast_in_dim_reshape.10), channel_id=1, source_target_pairs={{0,16},{4,20},{8,24},{12,28},{16,0},{20,4},{24,8},{28,12},{1,17},{... | collective-permute-start | bytes 221192 | tf_op jit(solution)/shard_map/ppermute | solution.py:257
  33.2 55.0 %collective-permute-start.27 = (bf16[384,768]{1,0:T(8,128)(2,1)S(1)}, bf16[384,768]{1,0:T(8,128)(2,1)S(1)}, u32[]{:S(2)}, u32[]{:S(2)}) collective-permute-start(bf16[384,768]{1,0:T(8,128)(2,1)S(1)} %copy-done.29), channel_id=1, source_target_pairs={{0,16},{2,18},{4,20},{6,22},{8,24},{10,26},{12,28},{14,30},{17,1},... | collective-permute-start | bytes 1769480 | tf_op jit(solution)/shard_map/ppermute | solution.py:271
  34.8 45.9 %collective-permute-start.3 = (bf16[512,768]{1,0:T(8,128)(2,1)S(1)}, bf16[512,768]{1,0:T(8,128)(2,1)S(1)}, u32[]{:S(2)}, u32[]{:S(2)}) collective-permute-start(bf16[512,768]{1,0:T(8,128)(2,1)S(1)} %copy-done.8), channel_id=1, source_target_pairs={{0,1},{1,0},{2,3},{3,2},{4,5},{5,4},{6,7},{7,6},{8,9},{9,8},{10,11... | collective-permute-start | bytes 2359304 | tf_op jit(solution)/shard_map/ppermute | solution.py:260
  61.0 19.5 %collective-permute-start.2 = (bf16[4,96,384]{2,1,0:T(8,128)(2,1)S(1)}, bf16[4,96,384]{2,1,0:T(8,128)(2,1)S(1)}, u32[]{:S(2)}, u32[]{:S(2)}) collective-permute-start(bf16[4,96,384]{2,1,0:T(8,128)(2,1)S(1)} %bitcast.590), channel_id=1, source_target_pairs={{0,4},{4,0},{8,12},{12,8},{16,20},{20,16},{24,28},{28,24},{1,5},{5... | collective-permute-start | bytes 884744 | tf_op jit(solution)/shard_map/ppermute | solution.py:257
  67.9 22.2 %collective-permute-start.18 = (bf16[2,96,768]{2,1,0:T(8,128)(2,1)S(1)}, bf16[2,96,768]{2,1,0:T(8,128)(2,1)S(1)}, u32[]{:S(2)}, u32[]{:S(2)}) collective-permute-start(bf16[2,96,768]{2,1,0:T(8,128)(2,1)S(1)} %maximum_select_fusion.24), channel_id=1, source_target_pairs={{0,4},{4,0},{8,12},{12,8},{16,20},{20,16},{24,28},{28,24},{1,5},{5... | collective-permute-start | bytes 884744 | tf_op jit(solution)/shard_map/ppermute | solution.py:257
  74.2 97.2 %collective-permute-start.25 = (bf16[2,96,1536]{2,1,0:T(8,128)(2,1)}, bf16[2,96,1536]{2,1,0:T(8,128)(2,1)}, u32[]{:S(2)}, u32[]{:S(2)}) collective-permute-start(bf16[2,96,1536]{2,1,0:T(8,128)(2,1)} %maximum_select_fusion.17), channel_id=1, source_target_pairs={{0,8},{4,12},{8,0},{12,4},{16,24},{20,28},{24,16},{28,20},{1,9},{5... | collective-permute-start | bytes 1769480 | tf_op jit(solution)/shard_map/ppermute | solution.py:257
  82.8 61.5 %collective-permute-start.14 = (bf16[192,1024]{1,0:T(8,128)(2,1)}, bf16[192,1024]{1,0:T(8,128)(2,1)}, u32[]{:S(2)}, u32[]{:S(2)}) collective-permute-start(bf16[192,1024]{1,0:T(8,128)(2,1)} %bitcast.42), channel_id=1, source_target_pairs={{0,2},{1,3},{2,0},{3,1},{4,6},{5,7},{6,4},{7,5},{8,10},{9,11},{10,... | collective-permute-start | bytes 1179656 | tf_op jit(solution)/shard_map/ppermute | solution.py:263
  86.3 40.2 %collective-permute-start.9 = (bf16[192,1024]{1,0:T(8,128)(2,1)}, bf16[192,1024]{1,0:T(8,128)(2,1)}, u32[]{:S(2)}, u32[]{:S(2)}) collective-permute-start(bf16[192,1024]{1,0:T(8,128)(2,1)} %bitcast.29), channel_id=1, source_target_pairs={{0,2},{1,3},{2,0},{3,1},{4,6},{5,7},{6,4},{7,5},{8,10},{9,11},{10,... | collective-permute-start | bytes 1179656 | tf_op jit(solution)/shard_map/ppermute | solution.py:263
  88.2 18.4 %collective-permute-start.4 = (bf16[192,1024]{1,0:T(8,128)(2,1)S(1)}, bf16[192,1024]{1,0:T(8,128)(2,1)S(1)}, u32[]{:S(2)}, u32[]{:S(2)}) collective-permute-start(bf16[192,1024]{1,0:T(8,128)(2,1)S(1)} %bitcast.615), channel_id=1, source_target_pairs={{0,2},{1,3},{2,0},{3,1},{4,6},{5,7},{6,4},{7,5},{8,10},{9,11},{10,... | collective-permute-start | bytes 1179656 | tf_op jit(solution)/shard_map/ppermute | solution.py:263
  90.1 82.8 %collective-permute-start.28 = (bf16[1,384,768]{2,1,0:T(8,128)(2,1)S(1)}, bf16[1,384,768]{2,1,0:T(8,128)(2,1)S(1)}, u32[]{:S(2)}, u32[]{:S(2)}) collective-permute-start(bf16[1,384,768]{2,1,0:T(8,128)(2,1)S(1)} %get-tuple-element.69), channel_id=1, source_target_pairs={{0,8},{4,12},{8,0},{12,4},{16,24},{20,28},{24,16},{28,20},{1,9},{5... | collective-permute-start | bytes 1769480 | tf_op jit(solution)/shard_map/ppermute | solution.py:257
  124.8 39.0 %collective-permute-start.5 = (bf16[64,1024]{1,0:T(8,128)(2,1)}, bf16[64,1024]{1,0:T(8,128)(2,1)}, u32[]{:S(2)}, u32[]{:S(2)}) collective-permute-start(bf16[64,1024]{1,0:T(8,128)(2,1)} %get-tuple-element.29), channel_id=1, source_target_pairs={{0,2},{1,3},{2,0},{3,1},{4,6},{5,7},{6,4},{7,5},{8,10},{9,11},{10,... | collective-permute-start | bytes 393224 | tf_op jit(solution)/shard_map/ppermute | solution.py:263
  143.9 21.0 %collective-permute-start.10 = (bf16[64,1024]{1,0:T(8,128)(2,1)}, bf16[64,1024]{1,0:T(8,128)(2,1)}, u32[]{:S(2)}, u32[]{:S(2)}) collective-permute-start(bf16[64,1024]{1,0:T(8,128)(2,1)} %get-tuple-element.31), channel_id=1, source_target_pairs={{0,2},{1,3},{2,0},{3,1},{4,6},{5,7},{6,4},{7,5},{8,10},{9,11},{10,... | collective-permute-start | bytes 393224 | tf_op jit(solution)/shard_map/ppermute | solution.py:263
  172.8 28.9 %collective-permute-start.26 = (bf16[4,96,1536]{2,1,0:T(8,128)(2,1)S(1)}, bf16[4,96,1536]{2,1,0:T(8,128)(2,1)S(1)}, u32[]{:S(2)}, u32[]{:S(2)}) collective-permute-start(bf16[4,96,1536]{2,1,0:T(8,128)(2,1)S(1)} %bitcast.531), channel_id=1, source_target_pairs={{0,4},{4,0},{8,12},{12,8},{16,20},{20,16},{24,28},{28,24},{1,5},{5... | collective-permute-start | bytes 3538952 | tf_op jit(solution)/shard_map/ppermute | solution.py:257
  173.1 52.7 %collective-permute-start.29 = (bf16[2,384,768]{2,1,0:T(8,128)(2,1)S(1)}, bf16[2,384,768]{2,1,0:T(8,128)(2,1)S(1)}, u32[]{:S(2)}, u32[]{:S(2)}) collective-permute-start(bf16[2,384,768]{2,1,0:T(8,128)(2,1)S(1)} %maximum_select_fusion.8), channel_id=1, source_target_pairs={{0,4},{4,0},{8,12},{12,8},{16,20},{20,16},{24,28},{28,24},{1,5},{5... | collective-permute-start | bytes 3538952 | tf_op jit(solution)/shard_map/ppermute | solution.py:257
  176.4 49.7 %collective-permute-start.23 = (bf16[512,768]{1,0:T(8,128)(2,1)S(1)}, bf16[512,768]{1,0:T(8,128)(2,1)S(1)}, u32[]{:S(2)}, u32[]{:S(2)}) collective-permute-start(bf16[512,768]{1,0:T(8,128)(2,1)S(1)} %fusion.18), channel_id=1, source_target_pairs={{0,1},{1,0},{2,3},{3,2},{4,5},{5,4},{6,7},{7,6},{8,9},{9,8},{10,11... | collective-permute-start | bytes 2359304 | tf_op jit(solution)/shard_map/ppermute | solution.py:260
  273.3 28.9 %collective-permute-start.62 = (bf16[2,384,768]{2,1,0:T(8,128)(2,1)S(1)}, bf16[2,384,768]{2,1,0:T(8,128)(2,1)S(1)}, u32[]{:S(2)}, u32[]{:S(2)}) collective-permute-start(bf16[2,384,768]{2,1,0:T(8,128)(2,1)S(1)} %select_bitcast_fusion), channel_id=1, source_target_pairs={{0,4},{4,0},{8,12},{12,8},{16,20},{20,16},{24,28},{28,24},{1,5},{5... | collective-permute-start | bytes 3538952 | tf_op jit(solution)/shard_map/ppermute | solution.py:257
  275.1 51.5 %collective-permute-start.57 = (bf16[4,96,1536]{2,1,0:T(8,128)(2,1)S(1)}, bf16[4,96,1536]{2,1,0:T(8,128)(2,1)S(1)}, u32[]{:S(2)}, u32[]{:S(2)}) collective-permute-start(bf16[4,96,1536]{2,1,0:T(8,128)(2,1)S(1)} %select_bitcast_fusion.1), channel_id=1, source_target_pairs={{0,4},{4,0},{8,12},{12,8},{16,20},{20,16},{24,28},{28,24},{1,5},{5... | collective-permute-start | bytes 3538952 | tf_op jit(solution)/shard_map/ppermute | solution.py:257
  287.1 40.1 %collective-permute-start.33 = (bf16[512,768]{1,0:T(8,128)(2,1)S(1)}, bf16[512,768]{1,0:T(8,128)(2,1)S(1)}, u32[]{:S(2)}, u32[]{:S(2)}) collective-permute-start(bf16[512,768]{1,0:T(8,128)(2,1)S(1)} %get-tuple-element.60), channel_id=1, source_target_pairs={{0,1},{1,0},{2,3},{3,2},{4,5},{5,4},{6,7},{7,6},{8,9},{9,8},{10,11... | collective-permute-start | bytes 2359304 | tf_op jit(solution)/shard_map/ppermute | solution.py:260
  302.7 31.9 %collective-permute-start.63 = (bf16[1,384,768]{2,1,0:T(8,128)(2,1)S(1)}, bf16[1,384,768]{2,1,0:T(8,128)(2,1)S(1)}, u32[]{:S(2)}, u32[]{:S(2)}) collective-permute-start(bf16[1,384,768]{2,1,0:T(8,128)(2,1)S(1)} %select_bitcast_fusion.2), channel_id=1, source_target_pairs={{0,8},{4,12},{8,0},{12,4},{16,24},{20,28},{24,16},{28,20},{1,9},{5... | collective-permute-start | bytes 1769480 | tf_op jit(solution)/shard_map/ppermute | solution.py:257
  335.6 97.8 %collective-permute-start.64 = (bf16[384,768]{1,0:T(8,128)(2,1)}, bf16[384,768]{1,0:T(8,128)(2,1)}, u32[]{:S(2)}, u32[]{:S(2)}) collective-permute-start(bf16[384,768]{1,0:T(8,128)(2,1)} %fusion.24), channel_id=1, source_target_pairs={{1,17},{3,19},{5,21},{7,23},{9,25},{11,27},{13,29},{15,31},{16,0},... | collective-permute-start | bytes 1769480 | tf_op jit(solution)/shard_map/ppermute | solution.py:271
  341.9 69.9 %collective-permute-start.59 = (bf16[1,96,1536]{2,1,0:T(8,128)(2,1)S(1)}, bf16[1,96,1536]{2,1,0:T(8,128)(2,1)S(1)}, u32[]{:S(2)}, u32[]{:S(2)}) collective-permute-start(bf16[1,96,1536]{2,1,0:T(8,128)(2,1)S(1)} %select_bitcast_fusion.4), channel_id=1, source_target_pairs={{0,16},{4,20},{8,24},{12,28},{16,0},{20,4},{24,8},{28,12},{1,17},{... | collective-permute-start | bytes 884744 | tf_op jit(solution)/shard_map/ppermute | solution.py:257
  345.6 43.6 %collective-permute-start.53 = (bf16[1,96,768]{2,1,0:T(8,128)(2,1)S(1)}, bf16[1,96,768]{2,1,0:T(8,128)(2,1)S(1)}, u32[]{:S(2)}, u32[]{:S(2)}) collective-permute-start(bf16[1,96,768]{2,1,0:T(8,128)(2,1)S(1)} %select_bitcast_fusion.9), channel_id=1, source_target_pairs={{0,8},{4,12},{8,0},{12,4},{16,24},{20,28},{24,16},{28,20},{1,9},{5... | collective-permute-start | bytes 442376 | tf_op jit(solution)/shard_map/ppermute | solution.py:257
  367.7 56.7 %collective-permute-start.36 = (bf16[192,1024]{1,0:T(8,128)(2,1)}, bf16[192,1024]{1,0:T(8,128)(2,1)S(1)}, u32[]{:S(2)}, u32[]{:S(2)}) collective-permute-start(bf16[192,1024]{1,0:T(8,128)(2,1)} %get-tuple-element.41), channel_id=1, source_target_pairs={{0,2},{1,3},{2,0},{3,1},{4,6},{5,7},{6,4},{7,5},{8,10},{9,11},{10,... | collective-permute-start | bytes 1179656 | tf_op jit(solution)/shard_map/ppermute | solution.py:263
  389.3 39.7 %collective-permute-start.37 = (bf16[192,1024]{1,0:T(8,128)(2,1)}, bf16[192,1024]{1,0:T(8,128)(2,1)S(1)}, u32[]{:S(2)}, u32[]{:S(2)}) collective-permute-start(bf16[192,1024]{1,0:T(8,128)(2,1)} %get-tuple-element.45), channel_id=1, source_target_pairs={{0,2},{1,3},{2,0},{3,1},{4,6},{5,7},{6,4},{7,5},{8,10},{9,11},{10,... | collective-permute-start | bytes 1179656 | tf_op jit(solution)/shard_map/ppermute | solution.py:263
  389.4 20.3 %collective-permute-start.54 = (bf16[96,768]{1,0:T(8,128)(2,1)S(1)}, bf16[96,768]{1,0:T(8,128)(2,1)S(1)}, u32[]{:S(2)}, u32[]{:S(2)}) collective-permute-start(bf16[96,768]{1,0:T(8,128)(2,1)S(1)} %fusion.44), channel_id=1, source_target_pairs={{1,17},{3,19},{5,21},{7,23},{9,25},{11,27},{13,29},{15,31},{16,0},... | collective-permute-start | bytes 442376 | tf_op jit(solution)/shard_map/ppermute | solution.py:271
  409.7 17.0 %collective-permute-start.35 = (bf16[192,1024]{1,0:T(8,128)(2,1)}, bf16[192,1024]{1,0:T(8,128)(2,1)S(1)}, u32[]{:S(2)}, u32[]{:S(2)}) collective-permute-start(bf16[192,1024]{1,0:T(8,128)(2,1)} %get-tuple-element.37), channel_id=1, source_target_pairs={{0,2},{1,3},{2,0},{3,1},{4,6},{5,7},{6,4},{7,5},{8,10},{9,11},{10,... | collective-permute-start | bytes 1179656 | tf_op jit(solution)/shard_map/ppermute | solution.py:263
  433.4 16.6 %collective-permute-start.47 = (bf16[4,96,384]{2,1,0:T(8,128)(2,1)S(1)}, bf16[4,96,384]{2,1,0:T(8,128)(2,1)S(1)}, u32[]{:S(2)}, u32[]{:S(2)}) collective-permute-start(bf16[4,96,384]{2,1,0:T(8,128)(2,1)S(1)} %select_bitcast_fusion.6), channel_id=1, source_target_pairs={{0,4},{4,0},{8,12},{12,8},{16,20},{20,16},{24,28},{28,24},{1,5},{5... | collective-permute-start | bytes 884744 | tf_op jit(solution)/shard_map/ppermute | solution.py:257
  436.5 37.5 %collective-permute-start.65 = (bf16[384,768]{1,0:T(8,128)(2,1)}, bf16[384,768]{1,0:T(8,128)(2,1)}, u32[]{:S(2)}, u32[]{:S(2)}) collective-permute-start(bf16[384,768]{1,0:T(8,128)(2,1)} %add_convert_fusion.2), channel_id=1, source_target_pairs={{0,2},{1,3},{2,0},{3,1},{4,6},{5,7},{6,4},{7,5},{8,10},{9,11},{10,... | collective-permute-start | bytes 1769480 | tf_op jit(solution)/shard_map/ppermute | solution.py:263
  438.4 38.8 %collective-permute-start.38 = (bf16[512,768]{1,0:T(8,128)(2,1)}, bf16[512,768]{1,0:T(8,128)(2,1)}, u32[]{:S(2)}, u32[]{:S(2)}) collective-permute-start(bf16[512,768]{1,0:T(8,128)(2,1)} %select_convert_fusion), channel_id=1, source_target_pairs={{0,1},{1,0},{2,3},{3,2},{4,5},{5,4},{6,7},{7,6},{8,9},{9,8},{10,11... | collective-permute-start | bytes 2359304 | tf_op jit(solution)/shard_map/ppermute | solution.py:260
  (79 other events, 737.2 us)

commit v2 on v1

v2 whole, which is shorter than its diff:
```python
from functools import partial

import jax
import jax.numpy as jnp
from jax import lax
from jax.experimental import pallas as pl
from jax.experimental.pallas import tpu as pltpu
from jax.sharding import PartitionSpec as P

HEADS = 12
HEAD_DIM = 64
TRIO = 3 * HEAD_DIM
GROUPS = 16
EPSILON = 1e-12
FAR = -(2.0**30)
SCALE = HEAD_DIM**-0.5
TILE = 512
BF = jnp.bfloat16
F32 = jnp.float32
VMEM = pl.BlockSpec(memory_space=pltpu.VMEM)
SMEM = pl.BlockSpec(memory_space=pltpu.SMEM)
FREE = pl.CostEstimate(flops=1, bytes_accessed=1, transcendentals=0)


def dot(a, b, ca, cb):
    return lax.dot_general(a, b, (((ca,), (cb,)), ((), ())), preferred_element_type=F32)


def shape(dims, kind):
    return jax.ShapeDtypeStruct(dims, kind)


def params(mebi):
    return pltpu.CompilerParams(vmem_limit_bytes=mebi << 20)


def assemble_kernel(offsets, info, *refs):
    out = refs[-1]
    for ref, rel in zip(refs[:-1], offsets):
        block = ref.shape[1]
        for i, r in enumerate(rel):
            at = pl.multiple_of((info[0] ^ r) * block, block)
            out[pl.ds(at, block), :] = ref[i]


def assemble(pieces, offsets, me):
    block, cols = pieces[0].shape[1:]
    count = sum(len(r) for r in offsets)
    if block % 16:
        value = jnp.concatenate(pieces)
        order = [r for rel in offsets for r in rel]
        place = jnp.array([order.index(r) for r in range(count)], jnp.int32)
        return value[place[me ^ jnp.arange(count)]].reshape(count * block, cols)
    return pl.pallas_call(
        partial(assemble_kernel, offsets),
        out_shape=shape((count * block, cols), BF),
        in_specs=[SMEM] + [VMEM] * len(pieces),
        out_specs=VMEM,
        compiler_params=params(12),
        cost_estimate=FREE,
        name="assemble",
    )(me[None], *pieces)


def prepare_kernel(info, qkv, out_weight, *refs):
    vectors, (part_a, part_b, scratch) = refs[:4], refs[4:]
    block, width = out_weight.shape
    half, quarter = width // 2, width // 4
    scratch[...] = jnp.zeros_like(scratch)
    for i, ref in enumerate(vectors):
        scratch[i : i + 1, :block] = ref[...].astype(F32)
    part_a[:, TRIO:] = scratch[...].T[:block, : 256 - TRIO].astype(BF)
    for x in range(2):
        for c in range(2):

            @pl.when(jnp.logical_and(info[0] == x, info[1] == c))
            def _():
                at = c * half + x * quarter
                trio = [qkv[:, i * width + at : i * width + at + quarter] for i in range(3)]
                for j in range(3):
                    piece = jnp.concatenate(
                        [t[:, j * HEAD_DIM : (j + 1) * HEAD_DIM] for t in trio], 1
                    )
                    if j == 0:
                        part_a[:, :TRIO] = piece
                    else:
                        part_b[:, (j - 1) * TRIO : j * TRIO] = piece
                part_b[:, 2 * TRIO :] = out_weight[:, c * half : (c + 1) * half]


def prepare(info, qkv, out_weight, vectors):
    block, width = out_weight.shape
    return pl.pallas_call(
        prepare_kernel,
        out_shape=(shape((block, 256), BF), shape((block, 2 * TRIO + width // 2), BF)),
        in_specs=[SMEM] + [VMEM] * 6,
        out_specs=(VMEM, VMEM),
        scratch_shapes=[pltpu.VMEM((128, 128), F32)],
        compiler_params=params(8),
        cost_estimate=FREE,
        name="prepare",
    )(info, qkv, out_weight, *[v[None] for v in vectors])


def vectors_kernel(part, out):
    out[...] = part[:, 128:].astype(F32).T[TRIO - 128 : TRIO - 120]


def vectors_of(part):
    return pl.pallas_call(
        vectors_kernel,
        out_shape=shape((8, part.shape[0]), F32),
        in_specs=[VMEM],
        out_specs=VMEM,
        compiler_params=params(8),
        cost_estimate=FREE,
        name="vectors",
    )(part)


def doc_rows(ids_ref, same, other):
    ids = ids_ref[...]
    rows = lax.broadcasted_iota(jnp.int32, (GROUPS, ids.shape[1]), 0)
    return jnp.where(rows == ids, same, other).astype(BF)


def tile_at(index, me):
    return pl.multiple_of((index ^ me) * TILE, TILE)


def attend_kernel(
    info, tok0, tok1, tok2, tok3, weight, ids_ref, ctx_own, ctx_send, ctx_full, lse,
    q_t, k_nat, v_t, s_ref,
):
    total = ids_ref.shape[1]
    half = total // 2
    tiles = total // TILE
    me = info[2 * tiles]
    weight_t = weight[...].T
    keys = weight[:, HEAD_DIM : 2 * HEAD_DIM]
    for i, tok in enumerate((tok0, tok1, tok2, tok3)):
        at = i * TILE
        rows = tok[...]
        trio = dot(weight_t, rows, 1, 1).astype(BF)
        q_t[:HEAD_DIM, at : at + TILE] = trio[:HEAD_DIM] * SCALE
        v_t[:, at : at + TILE] = trio[2 * HEAD_DIM :]
        k_nat[at : at + TILE, :HEAD_DIM] = dot(rows, keys, 1, 0).astype(BF)
    q_t[HEAD_DIM : HEAD_DIM + GROUPS, :] = doc_rows(ids_ref, 0.0, FAR)
    q_t[HEAD_DIM + GROUPS :, :] = jnp.zeros((128 - HEAD_DIM - GROUPS, total), BF)
    docs = jnp.concatenate(
        [doc_rows(ids_ref, 1.0, 0.0), jnp.zeros((128 - HEAD_DIM - GROUPS, total), BF)], 0
    )
    k_nat[:, HEAD_DIM:] = docs.T

    def query_tile(i, carry):
        at = tile_at(i, me)
        query = q_t[:, pl.ds(at, TILE)]
        begin, end = info[i], info[tiles + i]

        def score(k, top):
            scores = dot(k_nat[pl.ds(tile_at(k, me), TILE), :], query, 1, 0)
            s_ref[pl.ds(pl.multiple_of(k * TILE, TILE), TILE), :] = scores
            return jnp.maximum(top, jnp.max(scores.reshape(TILE // 8, 8, TILE), 0))

        top = lax.fori_loop(begin, end, score, jnp.full((8, TILE), -3e38, F32))
        top = jnp.max(top, 0, keepdims=True)

        def weigh(k, state):
            total8, acc = state
            powers = jnp.exp(s_ref[pl.ds(pl.multiple_of(k * TILE, TILE), TILE), :] - top)
            total8 = total8 + jnp.sum(powers.reshape(TILE // 8, 8, TILE), 0)
            acc = acc + dot(v_t[:, pl.ds(tile_at(k, me), TILE)], powers.astype(BF), 1, 0)
            return total8, acc

        total8, acc = lax.fori_loop(
            begin, end, weigh, (jnp.zeros((8, TILE), F32), jnp.zeros((HEAD_DIM, TILE), F32))
        )
        sums = jnp.sum(total8, 0, keepdims=True)
        ctx_full[:, pl.ds(at, TILE)] = acc / sums
        lse[:, pl.ds(at, TILE)] = top + jnp.log(sums)
        return carry

    lax.fori_loop(0, tiles, query_tile, 0)
    ctx_own[...] = ctx_full[:, :half].astype(BF)
    ctx_send[...] = ctx_full[:, half:].astype(BF)


def attend(info, toks, weight, ids):
    total = ids.shape[1]
    half = total // 2
    return pl.pallas_call(
        attend_kernel,
        out_shape=(
            shape((HEAD_DIM, half), BF),
            shape((HEAD_DIM, half), BF),
            shape((HEAD_DIM, total), F32),
            shape((1, total), F32),
        ),
        in_specs=[SMEM] + [VMEM] * 6,
        out_specs=(VMEM,) * 4,
        scratch_shapes=[
            pltpu.VMEM((128, total), BF),
            pltpu.VMEM((total, 128), BF),
            pltpu.VMEM((HEAD_DIM, total), BF),
            pltpu.VMEM((total, TILE), F32),
        ],
        compiler_params=params(24),
        cost_estimate=FREE,
        name="attend",
    )(info, *toks, weight, ids)


def attend_back_kernel(
    order, info, tok0, tok1, tok2, tok3, weight, ids_ref, g_own, g_recv, ctx_full, lse, sums,
    out, grad_out, q_t, kvd, k_t, g_t, qg_nat, acc, dq_t, w_grad,
):
    total = ids_ref.shape[1]
    half = total // 2
    tiles = total // TILE
    me, shard = info[2 * tiles], info[2 * tiles + 1]
    toks = (tok0, tok1, tok2, tok3)
    weight_t = weight[:, : 2 * HEAD_DIM].T
    natural_w = weight[:, HEAD_DIM:]
    for at, grad in ((0, g_own), (half, g_recv)):
        g_t[HEAD_DIM:, at : at + half] = grad[...]
    g_t[:HEAD_DIM, :] = jnp.zeros((HEAD_DIM, total), BF)
    for i, tok in enumerate(toks):
        at = i * TILE
        rows = tok[...]
        pair = dot(weight_t, rows, 1, 1).astype(BF)
        q_t[:HEAD_DIM, at : at + TILE] = pair[:HEAD_DIM] * SCALE
        k_t[:, at : at + TILE] = pair[HEAD_DIM:]
        kvd[at : at + TILE, :128] = dot(rows, natural_w, 1, 0).astype(BF)
    qg_nat[...] = jnp.concatenate([q_t[:HEAD_DIM, :], g_t[HEAD_DIM:, :]], 0).T
    q_t[HEAD_DIM:128, :] = jnp.zeros((128 - HEAD_DIM, total), BF)
    q_t[128 : 128 + GROUPS, :] = doc_rows(ids_ref, 0.0, FAR)
    q_t[128 + GROUPS :, :] = jnp.zeros((128 - GROUPS, total), BF)
    kvd[:, 128:] = jnp.concatenate(
        [doc_rows(ids_ref, 1.0, 0.0), jnp.zeros((128 - GROUPS, total), BF)], 0
    ).T
    acc[...] = jnp.zeros_like(acc)

    def query_tile(i, carry):
        at = tile_at(i, me)
        query = q_t[:, pl.ds(at, TILE)]
        grad = g_t[:, pl.ds(at, TILE)]
        row_term = jnp.sum(
            ctx_full[:, pl.ds(at, TILE)] * grad[HEAD_DIM:].astype(F32), 0, keepdims=True
        )
        log_total = lse[:, pl.ds(at, TILE)]
        natural = qg_nat[pl.ds(at, TILE), :]
        left = lax.broadcasted_iota(jnp.int32, (TILE, 128), 1) < HEAD_DIM

        def key_tile(k, dq):
            kat = tile_at(k, me)
            scores = dot(kvd[pl.ds(kat, TILE), :], query, 1, 0)
            chance = jnp.exp(scores - log_total)
            grad_chance = dot(kvd[pl.ds(kat, TILE), :128], grad, 1, 0)
            grad_scores = (chance * (grad_chance - row_term)).astype(BF)
            dq = dq + dot(k_t[:, pl.ds(kat, TILE)], grad_scores, 1, 0)
            acc[pl.ds(kat, TILE), :] += jnp.where(
                left, dot(grad_scores, natural, 1, 0), dot(chance.astype(BF), natural, 1, 0)
            )
            return dq

        dq = lax.fori_loop(info[i], info[tiles + i], key_tile, jnp.zeros((HEAD_DIM, TILE), F32))
        dq_t[:, pl.ds(at, TILE)] = (dq * SCALE).astype(BF)
        return carry

    lax.fori_loop(0, tiles, query_tile, 0)
    out[:HEAD_DIM, :] = dq_t[...]
    out[HEAD_DIM:, :] = acc[...].T.astype(BF)
    for i, tok in enumerate(toks):
        part = dot(out[:, i * TILE : (i + 1) * TILE], tok[...], 1, 0)
        w_grad[:TRIO, :] = part if i == 0 else w_grad[:TRIO, :] + part
    if sums is not None:
        w_grad[TRIO : TRIO + 8, :] = sums[...]
        w_grad[TRIO + 8 :, :] = jnp.zeros((256 - TRIO - 8, w_grad.shape[1]), F32)
    else:
        w_grad[TRIO:, :] = jnp.zeros((256 - TRIO, w_grad.shape[1]), F32)
    natural = w_grad[...].T
    block = grad_out.shape[1]
    for b in range(len(order)):
        grad_out[order_of(order, shard, b)] = natural[b * block : (b + 1) * block].astype(BF)


def order_of(order, me, b):
    rel = me ^ b
    bits = len(order).bit_length() - 1
    place = 0
    for i in range(bits):
        place = place | (((rel >> i) & 1) << (bits - 1 - i))
    return place


def attend_back(info, toks, weight, ids, g_own, g_recv, ctx_full, lse, sums, n_shard):
    total = ids.shape[1]
    width = weight.shape[0]
    extra = [] if sums is None else [sums]

    def kernel(*refs):
        refs = list(refs)
        if sums is None:
            refs.insert(11, None)
        attend_back_kernel(range(n_shard), *refs)

    return pl.pallas_call(
        kernel,
        out_shape=(shape((TRIO, total), BF), shape((n_shard, width // n_shard, 256), BF)),
        in_specs=[SMEM] + [VMEM] * (10 + len(extra)),
        out_specs=(VMEM, VMEM),
        scratch_shapes=[
            pltpu.VMEM((256, total), BF),
            pltpu.VMEM((total, 256), BF),
            pltpu.VMEM((HEAD_DIM, total), BF),
            pltpu.VMEM((128, total), BF),
            pltpu.VMEM((total, 128), BF),
            pltpu.VMEM((total, 128), F32),
            pltpu.VMEM((HEAD_DIM, total), BF),
            pltpu.VMEM((256, width), F32),
        ],
        compiler_params=params(24),
        cost_estimate=FREE,
        name="attend_back",
    )(info, *toks, weight, ids, g_own, g_recv, ctx_full, lse, *extra)


def input_back_kernel(d0, d1, d2, w0, w1, w2, own, over_x, send_core):
    rows = own.shape[0]
    weights = jnp.concatenate([w[...] for w in (w0, w1, w2)], 1)
    for r, out in enumerate((own, send_core.at[0], over_x, send_core.at[1])):
        at = r * rows
        grads = jnp.concatenate([d[:, at : at + rows] for d in (d0, d1, d2)], 0)
        out[...] = dot(grads.T, weights, 1, 1).astype(out.dtype)


def input_back(grads, weights, rows):
    width = weights[0].shape[0]
    return pl.pallas_call(
        input_back_kernel,
        out_shape=(
            shape((rows, width), F32), shape((rows, width), F32), shape((2, rows, width), BF)
        ),
        in_specs=[VMEM] * 6,
        out_specs=(VMEM,) * 3,
        compiler_params=params(24),
        cost_estimate=FREE,
        name="input_back",
    )(*grads, *weights)


def place_qkv_kernel(info, own, over_x, over_core, over_both, out, sums_out):
    part = out.shape[1] // 3
    quarter = part // 4
    x, c = info[0], info[1]
    total = None
    for ref, dx, dc in ((own, 0, 0), (over_x, 1, 0), (over_core, 0, 1), (over_both, 1, 1)):
        value = ref[...].astype(F32)
        tail = value[:, 2 * 256 + TRIO : 2 * 256 + TRIO + 8]
        total = tail if total is None else total + tail
        for sec in range(3):
            at = sec * HEAD_DIM
            piece = jnp.concatenate(
                [value[:, j * 256 + at : j * 256 + at + HEAD_DIM] for j in range(3)], 1
            )
            for xv in range(2):
                for cv in range(2):
                    to = sec * part + (cv * 2 + xv) * quarter

                    @pl.when(jnp.logical_and((x ^ dx) == xv, (c ^ dc) == cv))
                    def _():
                        out[:, to : to + quarter] = piece

    sums_out[...] = total


def place_qkv(info, own, over_x, over_core, over_both, width):
    block = own.shape[0]
    return pl.pallas_call(
        place_qkv_kernel,
        out_shape=(shape((block, 3 * width), F32), shape((block, 8), F32)),
        in_specs=[SMEM] + [VMEM] * 4,
        out_specs=(VMEM, VMEM),
        compiler_params=params(8),
        cost_estimate=FREE,
        name="place_qkv",
    )(info, own, over_x, over_core, over_both)


def gelu_both(u):
    root = 0.7978845608028654
    cube = 0.044715 * root
    square = u * u
    t = jnp.tanh(u * (root + cube * square))
    half = 0.5 * (1.0 + t)
    act = u * half
    slope = half + act * (1.0 - t) * (root + 3.0 * cube * square)
    return act, slope


def feed_up_kernel(low_own, low_other, up, act_out, act_t, slope_out, low_t):
    rows = low_own.shape[0]
    step = 256
    for p, low in enumerate((low_own, low_other)):

        def body(i, carry):
            at = pl.multiple_of(i * step, step)
            to = pl.multiple_of(p * rows + i * step, step)
            value = low[pl.ds(at, step), :]
            low_t[:, pl.ds(to, step)] = value.T
            act, slope = gelu_both(dot(value, up[...], 1, 0))
            act = act.astype(BF)
            act_out[pl.ds(to, step), :] = act
            act_t[:, pl.ds(to, step)] = act.T
            slope_out[pl.ds(to, step), :] = slope.astype(BF)
            return carry

        lax.fori_loop(0, rows // step, body, 0)


def feed_up(low_own, low_other, up):
    rows, width = low_own.shape
    hidden = up.shape[1]
    return pl.pallas_call(
        feed_up_kernel,
        out_shape=(
            shape((2 * rows, hidden), BF),
            shape((hidden, 2 * rows), BF),
            shape((2 * rows, hidden), BF),
            shape((width, 2 * rows), BF),
        ),
        in_specs=[VMEM] * 3,
        out_specs=(VMEM,) * 4,
        compiler_params=params(32),
        cost_estimate=FREE,
        name="feed_up",
    )(low_own, low_other, up)


def feed_down_kernel(act, down, own, send):
    rows = own.shape[0]
    step = 256
    for p, out in enumerate((own, send)):

        def body(i, carry):
            at = pl.multiple_of(i * step, step)
            value = act[pl.ds(pl.multiple_of(p * rows + i * step, step), step), :]
            out[pl.ds(at, step), :] = dot(value, down[...], 1, 0).astype(out.dtype)
            return carry

        lax.fori_loop(0, rows // step, body, 0)


def feed_down(act, down):
    rows, hidden = act.shape
    width = down.shape[1]
    return pl.pallas_call(
        feed_down_kernel,
        out_shape=(shape((rows // 2, width), F32), shape((rows // 2, width), BF)),
        in_specs=[VMEM] * 2,
        out_specs=(VMEM,) * 2,
        compiler_params=params(24),
        cost_estimate=FREE,
        name="feed_down",
    )(act, down)


def feed_back_kernel(grad_own, grad_other, slope, up, down, own, send, pre_out):
    rows = grad_own.shape[0]
    step = 256
    for p, (grad, out) in enumerate(((grad_own, own), (grad_other, send))):

        def body(i, carry):
            at = pl.multiple_of(i * step, step)
            to = pl.multiple_of(p * rows + i * step, step)
            pre = dot(grad[pl.ds(at, step), :], down[...], 1, 1)
            pre = (pre * slope[pl.ds(to, step), :].astype(F32)).astype(BF)
            pre_out[pl.ds(to, step), :] = pre
            out[pl.ds(at, step), :] = dot(pre, up[...], 1, 1).astype(out.dtype)
            return carry

        lax.fori_loop(0, rows // step, body, 0)


def feed_back(grad_own, grad_other, slope, up, down):
    rows, width = grad_own.shape
    hidden = up.shape[1]
    return pl.pallas_call(
        feed_back_kernel,
        out_shape=(
            shape((rows, width), F32),
            shape((rows, width), BF),
            shape((2 * rows, hidden), BF),
        ),
        in_specs=[VMEM] * 5,
        out_specs=(VMEM,) * 3,
        compiler_params=params(32),
        cost_estimate=FREE,
        name="feed_back",
    )(grad_own, grad_other, slope, up, down)


def weight_grad_kernel(blocks, shard, left, right_own, right_other, out):
    rows, cols = left.shape[0], out.shape[2]
    half = left.shape[1] // 2
    step = 256
    block = out.shape[1]
    lone = right_other is None

    def body(i, carry):
        at = pl.multiple_of(i * step, step)
        if lone:
            value = dot(left[...], right_own[:, pl.ds(at, step)], 1, 0)
        else:
            value = dot(left[:, :half], right_own[:, pl.ds(at, step)], 1, 0) + dot(
                left[:, half:], right_other[:, pl.ds(at, step)], 1, 0
            )
        for b in range(blocks):
            out[order_of(range(blocks), shard[0], b), :, pl.ds(at, step)] = value[
                b * block : (b + 1) * block
            ].astype(BF)
        return carry

    lax.fori_loop(0, cols // step, body, 0)


def weight_grad(shard, left, rights, blocks):
    rows, cols = left.shape[0], rights[0].shape[1]

    def kernel(*refs):
        refs = list(refs)
        if len(rights) == 1:
            refs.insert(3, None)
        weight_grad_kernel(blocks, *refs)

    return pl.pallas_call(
        kernel,
        out_shape=shape((blocks, rows // blocks, cols), BF),
        in_specs=[SMEM, VMEM] + [VMEM] * len(rights),
        out_specs=VMEM,
        compiler_params=params(24),
        cost_estimate=FREE,
        name="weight_grad",
    )(shard[None], left, *rights)


def mix_back_kernel(info, mixer, context, grad_own, grad_other, g_own, g_send, own, send):
    quarter = g_own.shape[0]
    rows = grad_own.shape[0]
    half_width = own.shape[1]
    for p, grad in enumerate((grad_own, grad_other)):
        value = dot(mixer[...], grad[...], 1, 1).astype(BF)
        g_own[:, p * rows : (p + 1) * rows] = value[:quarter]
        g_send[:, p * rows : (p + 1) * rows] = value[quarter:]
    for out, half in ((own, info[1]), (send, 1 - info[1])):
        at = pl.multiple_of(half * half_width, half_width)
        out[...] = (
            dot(context[:, :rows], grad_own[:, pl.ds(at, half_width)], 1, 0)
            + dot(context[:, rows:], grad_other[:, pl.ds(at, half_width)], 1, 0)
        ).astype(BF)


def mix_back(info, mixer, context, grad_own, grad_other):
    half_width, width = mixer.shape
    rows = grad_own.shape[0]
    return pl.pallas_call(
        mix_back_kernel,
        out_shape=(shape((half_width // 2, 2 * rows), BF),) * 2
        + (shape((half_width, half_width), BF),) * 2,
        in_specs=[SMEM] + [VMEM] * 4,
        out_specs=(VMEM,) * 4,
        compiler_params=params(16),
        cost_estimate=FREE,
        name="mix_back",
    )(info, mixer, context, grad_own, grad_other)


def mix_place_kernel(blocks, info, own, recv, out, scratch):
    half_width = own.shape[1]
    quarter = half_width // 2
    x, c, shard = info[0], info[1], info[2]
    for ref, dc in ((own, 0), (recv, 1)):
        for dx in range(2):
            at = pl.multiple_of((c ^ dc) * half_width + (x ^ dx) * quarter, quarter)
            scratch[pl.ds(at, quarter), :] = ref[dx * quarter : (dx + 1) * quarter, :].astype(F32)
    block = out.shape[1]
    for b in range(blocks):
        out[order_of(range(blocks), shard, b)] = scratch[b * block : (b + 1) * block, :].astype(BF)


def mix_place(info, own, recv, blocks):
    half_width = own.shape[1]
    return pl.pallas_call(
        partial(mix_place_kernel, blocks),
        out_shape=shape((blocks, 2 * half_width // blocks, half_width), BF),
        in_specs=[SMEM, VMEM, VMEM],
        out_specs=VMEM,
        scratch_shapes=[pltpu.VMEM((2 * half_width, half_width), F32)],
        compiler_params=params(8),
        cost_estimate=FREE,
        name="mix_place",
    )(info, own, recv)


def row_tiles(rows, step, body):
    lax.fori_loop(0, rows // step, lambda i, c: body(pl.ds(pl.multiple_of(i * step, step), step), c), 0)


def mean_of(value):
    return jnp.mean(value, -1, keepdims=True)


def first_norm_kernel(tokens, mixed, recv, vectors, low, normed_out, inverse_out):
    gain, bias = vectors[0:1, :], vectors[1:2, :]

    def body(at, carry):
        hidden = tokens[at, :].astype(F32) + mixed[at, :] + recv[at, :].astype(F32)
        centred = hidden - mean_of(hidden)
        inverse = lax.rsqrt(mean_of(centred * centred) + EPSILON)
        normed = centred * inverse
        normed_out[at, :] = normed
        inverse_out[at, :] = inverse
        low[at, :] = (normed * gain + bias).astype(BF)
        return carry

    row_tiles(tokens.shape[0], 128, body)


def first_norm(tokens, mixed, recv, vectors):
    rows, width = tokens.shape
    return pl.pallas_call(
        first_norm_kernel,
        grid=(1,),
        out_shape=(shape((rows, width), BF), shape((rows, width), F32), shape((rows, 1), F32)),
        in_specs=[pl.BlockSpec((rows, width), lambda i: (0, 0))] * 3
        + [pl.BlockSpec(vectors.shape, lambda i: (0, 0))],
        out_specs=(pl.BlockSpec((rows, width), lambda i: (0, 0)),) * 2
        + (pl.BlockSpec((rows, 1), lambda i: (0, 0)),),
        compiler_params=params(24),
        cost_estimate=FREE,
        name="first_norm",
    )(tokens, mixed, recv, vectors)


def second_norm_kernel(normed_one, mlp, recv, vectors, grad, result, grad_two, grad_low, sums):
    gain_one, bias_one = vectors[0:1, :], vectors[1:2, :]
    gain, bias = vectors[2:3, :], vectors[3:4, :]
    sums[...] = jnp.zeros_like(sums)

    def body(at, carry):
        hidden = normed_one[at, :] * gain_one + bias_one + mlp[at, :] + recv[at, :].astype(F32)
        centred = hidden - mean_of(hidden)
        inverse = lax.rsqrt(mean_of(centred * centred) + EPSILON)
        normed = centred * inverse
        result[at, :] = (normed * gain + bias).astype(BF)
        grad_y = grad[at, :].astype(F32)
        grad_n = grad_y * gain
        value = inverse * (grad_n - mean_of(grad_n) - normed * mean_of(grad_n * normed))
        grad_two[at, :] = value
        grad_low[at, :] = value.astype(BF)
        sums[2:3, :] += jnp.sum(grad_y * normed, 0, keepdims=True)
        sums[3:4, :] += jnp.sum(grad_y, 0, keepdims=True)
        return carry

    row_tiles(grad.shape[0], 128, body)


def second_norm(normed_one, mlp, recv, vectors, grad):
    rows, width = grad.shape
    return pl.pallas_call(
        second_norm_kernel,
        out_shape=(
            shape((rows, width), BF),
            shape((rows, width), F32),
            shape((rows, width), BF),
            shape((8, width), F32),
        ),
        in_specs=[VMEM] * 5,
        out_specs=(VMEM,) * 4,
        compiler_params=params(24),
        cost_estimate=FREE,
        name="second_norm",
    )(normed_one, mlp, recv, vectors, grad)


def first_back_kernel(grad_two, own, recv, normed_one, inverse_one, vectors, late, grad_one, grad_low, sums):
    gain = vectors[0:1, :]
    sums[...] = late[...]

    def body(at, carry):
        normed = normed_one[at, :]
        grad_y = grad_two[at, :] + own[at, :] + recv[at, :].astype(F32)
        grad_n = grad_y * gain
        value = inverse_one[at, :] * (grad_n - mean_of(grad_n) - normed * mean_of(grad_n * normed))
        grad_one[at, :] = value
        grad_low[at, :] = value.astype(BF)
        sums[0:1, :] += jnp.sum(grad_y * normed, 0, keepdims=True)
        sums[1:2, :] += jnp.sum(grad_y, 0, keepdims=True)
        return carry

    row_tiles(grad_two.shape[0], 128, body)


def first_back(grad_two, own, recv, normed_one, inverse_one, vectors, late):
    rows, width = grad_two.shape
    return pl.pallas_call(
        first_back_kernel,
        out_shape=(shape((rows, width), F32), shape((rows, width), BF), shape((8, width), F32)),
        in_specs=[VMEM] * 7,
        out_specs=(VMEM,) * 3,
        compiler_params=params(24),
        cost_estimate=FREE,
        name="first_back",
    )(grad_two, own, recv, normed_one, inverse_one, vectors, late)


def after(value, *earlier):
    return lax.optimization_barrier((value,) + earlier)[0]


def shards(
    n_shard,
    tokens,
    segment_ids,
    qkv_weight,
    out_weight,
    up_weight,
    down_weight,
    first_gain,
    first_bias,
    second_gain,
    second_bias,
    out_grad,
):
    rows, width = tokens.shape
    half_width = width // 2
    quarter = width // 4
    ff_half = up_weight.shape[1] // 2
    block = qkv_weight.shape[0]
    shard = lax.axis_index("shard").astype(jnp.int32)
    seq = lax.axis_index("seq").astype(jnp.int32)
    xb, cb = seq // 2, seq % 2
    bits = [1 << b for b in range(n_shard.bit_length() - 1)]
    top = bits[-1]
    owner = (shard // top) % 2 == cb
    low_shard = shard % top
    place = jnp.stack([xb, cb, shard])

    def swap(value, mask):
        return lax.ppermute(value, "shard", [(i, i ^ mask) for i in range(n_shard)])

    def swap_core(value):
        return lax.ppermute(value, "seq", [(i, i ^ 1) for i in range(4)])

    def swap_x(value):
        return lax.ppermute(value, "seq", [(i, i ^ 2) for i in range(4)])

    def to_core(value, to_owner):
        pairs = []
        for sh in range(n_shard):
            for se in range(4):
                if (sh // top == se % 2) != to_owner:
                    pairs.append((sh * 4 + se, (sh ^ top) * 4 + se))
        return lax.ppermute(value, ("shard", "seq"), pairs)

    def join(pieces):
        return jnp.concatenate(pieces) if len(pieces) > 1 else pieces[0]

    class Gather:
        def __init__(self, own_block, over):
            self.pieces, self.offsets, self.over = [own_block[None]], [[0]], list(over)

        def swap(self, value, rel, bit):
            got = swap(value, bit)
            self.pieces.append(got)
            self.offsets.append([r ^ bit for r in rel])
            return got

        def steps(self, count, *gate):
            for bit in [self.over.pop(0) for _ in range(count)]:
                held, rel = join(self.pieces), [r for o in self.offsets for r in o]
                self.pieces, self.offsets = [held], [rel]
                gate = (self.swap(after(held, *gate), rel, bit),)
            return gate[0]

        def part(self, index, *gate):
            return self.swap(after(self.pieces[index], *gate), self.offsets[index], self.over[0])

    def fold(value, got):
        return (value[: value.shape[0] // 2].astype(F32) + got.astype(F32)).astype(BF)

    def upper(value):
        return value[value.shape[0] // 2 :]

    def add_x(value):
        return (value.astype(F32) + swap_x(value).astype(F32)).astype(BF)

    def pick(value, flag, axis):
        return jnp.where(
            flag == 0,
            lax.index_in_dim(value, 0, axis, False),
            lax.index_in_dim(value, 1, axis, False),
        )

    def ordered(flag, own, other, axis):
        return jnp.where(
            flag == 0, jnp.concatenate([own, other], axis), jnp.concatenate([other, own], axis)
        )

    over_x = swap_x(tokens)
    over_core = swap_core(tokens)
    toks = [tokens, over_core, over_x, swap_core(over_x)]
    ids = segment_ids[0]
    length = ids.shape[0]
    tiles = length // TILE
    first = ids.reshape(tiles, TILE)[:, 0]
    last = ids.reshape(tiles, TILE)[:, -1]
    begin = jnp.sum((ids[None] < first[:, None]).astype(jnp.int32), 1) // TILE
    end = (jnp.sum((ids[None] <= last[:, None]).astype(jnp.int32), 1) + TILE - 1) // TILE
    info = jnp.concatenate([begin, end, seq[None], shard[None]])
    chunks = ids.reshape(2, 2, 1, rows)
    chunks = jnp.where(xb == 0, chunks, chunks[::-1])
    chunks = jnp.where(cb == 0, chunks, chunks[:, ::-1])
    ids_row = chunks.reshape(1, length)

    own_a, own_b = prepare(
        place, qkv_weight, out_weight, (first_gain, first_bias, second_gain, second_bias)
    )
    up_half = lax.dynamic_slice_in_dim(up_weight, cb * ff_half, ff_half, 1)
    middle = len(bits) - 2
    gather_a = Gather(own_a, bits[::-1])
    gather_b = Gather(own_b, bits[::-1])
    gather_up = Gather(up_half, bits[::-1])
    a1 = gather_a.steps(1)
    b1 = gather_b.steps(1, a1)
    a2 = gather_a.steps(middle)
    a3 = gather_a.steps(1)
    b2 = gather_b.steps(middle, a2)
    u1 = gather_up.steps(1, b1)
    b3 = gather_b.steps(1, a3)
    down_there = to_core(after(down_weight, u1), False)
    part_a = assemble(gather_a.pieces, gather_a.offsets, shard)
    vectors = vectors_of(part_a)

    saved, own_ctx, other_ctx = [], [], []

    def head(j, weight, *gate):
        ctx_own, ctx_send, ctx_full, lse = attend(info, toks, weight, after(ids_row, *gate))
        own_ctx.append(ctx_own)
        other_ctx.append(swap_x(ctx_send))
        saved.append((ctx_full, lse))
        return ctx_own

    ctx = head(0, part_a[:, :TRIO], b2, vectors)
    u1, down_there = after(u1, ctx), after(down_there, ctx)
    gather_up.pieces[1] = u1
    gather_down = Gather(jnp.where(owner, down_weight, down_there), bits[-2::-1])
    u2 = gather_up.steps(middle, b2)
    ua = gather_up.part(0, b3)
    part_b = assemble(gather_b.pieces, gather_b.offsets, shard)
    ctx = head(1, part_b[:, :TRIO], u1, down_there)
    u2 = after(u2, ctx)
    gather_up.pieces[1] = u2
    d2 = gather_down.steps(middle, u2)
    ub = gather_up.part(1, ua)
    ctx = head(2, part_b[:, TRIO : 2 * TRIO], u2)
    d2 = after(d2, ctx)
    gather_down.pieces[1] = d2
    da = gather_down.part(0, ub)
    db = gather_down.part(1, da)
    widen = assemble(gather_up.pieces, gather_up.offsets, shard)
    narrow = assemble(gather_down.pieces, gather_down.offsets, low_shard)
    head_weights = [part_a[:, :TRIO], part_b[:, :TRIO], part_b[:, TRIO : 2 * TRIO]]
    mixer = part_b[:, 2 * TRIO :].reshape(2, half_width, half_width)
    mixer = ordered(cb, pick(mixer, cb, 0), swap_core(pick(mixer, 1 - cb, 0)), 1)
    mixer = jnp.where(xb == 0, mixer, jnp.concatenate([mixer[quarter:], mixer[:quarter]]))
    context = jnp.concatenate(own_ctx + other_ctx)

    mixed = dot(context, mixer, 0, 0)
    low_own, normed_one, inverse_one = first_norm(
        tokens, mixed, swap_core(mixed[rows:].astype(BF)), vectors
    )
    act_low, act_t, slope, low_t = feed_up(low_own, swap_core(low_own), widen)
    mlp_own, mlp_send = feed_down(act_low, narrow)
    result, grad_two, grad_mlp, late = second_norm(
        normed_one, mlp_own, swap_core(mlp_send), vectors, out_grad
    )

    grad_mlp = [grad_mlp, swap_core(grad_mlp)]
    narrow_grad = weight_grad(low_shard, act_t, grad_mlp, n_shard // 2)
    n1 = swap(upper(narrow_grad), bits[0])
    first_own, first_send, grad_pre = feed_back(
        after(grad_mlp[0], narrow_grad), grad_mlp[1], slope, widen, narrow
    )
    grad_one, grad_attn, sums = first_back(
        grad_two, first_own, swap_core(first_send), normed_one, inverse_one, vectors, late
    )
    g_own, g_send, mixer_own, mixer_send = mix_back(
        place, mixer, context, grad_attn, swap_core(grad_attn)
    )
    g_recv = swap_x(g_send)
    widen_grad = weight_grad(shard, after(low_t, g_send), [grad_pre], n_shard)
    w1 = swap(upper(widen_grad), bits[0])
    mixer_grad = mix_place(place, mixer_own, swap_core(mixer_send), n_shard)

    def head_back(j, *gate):
        at = j * HEAD_DIM
        return attend_back(
            info, toks, head_weights[j], after(ids_row, *gate),
            g_own[at : at + HEAD_DIM], g_recv[at : at + HEAD_DIM], *saved[j],
            sums if j == 2 else None, n_shard,
        )

    grads, parts = [None] * 3, [None] * 3
    narrow_grad = fold(narrow_grad, after(n1, widen_grad, mixer_grad))
    n2 = swap(upper(narrow_grad), bits[1])
    grads[0], parts[0] = head_back(0, narrow_grad)
    narrow_grad = fold(narrow_grad, after(n2, grads[0]))
    for bit in bits[2:-1]:
        narrow_grad = fold(narrow_grad, swap(upper(narrow_grad), bit))
    narrow_grad = narrow_grad[0]
    n3 = to_core(narrow_grad, True)
    grads[1], parts[1] = head_back(1, narrow_grad)
    widen_grad = fold(widen_grad, after(w1, grads[1]))
    w2 = swap(upper(widen_grad), bits[1])
    early = jnp.concatenate([mixer_grad, parts[0], parts[1]], 2)
    e1 = swap(upper(early), bits[0])
    narrow_grad = (narrow_grad.astype(F32) + after(n3, grads[1]).astype(F32)).astype(BF)
    n4 = swap_x(narrow_grad)
    grads[2], parts[2] = head_back(2, narrow_grad, widen_grad, early)
    late = parts[2]
    l1 = swap(upper(late), bits[0])
    widen_grad = fold(widen_grad, after(w2, grads[2]))
    for bit in bits[2:-1]:
        widen_grad = fold(widen_grad, swap(upper(widen_grad), bit))
    w3 = swap(upper(widen_grad), bits[-1])
    back_own, back_x, back_core = input_back(grads, head_weights, rows)
    back_recv = swap_core(back_core)
    back_x = (back_x + back_recv[1].astype(F32)).astype(BF)
    back_far = swap_x(back_x)
    early = fold(early, after(e1, back_x))
    e2 = swap(upper(early), bits[1])
    late = fold(late, after(l1, early))
    l2 = swap(upper(late), bits[1])
    early = fold(early, after(e2, late))
    for bit in bits[2:-1]:
        early = fold(early, swap(upper(early), bit))
    e3 = swap(upper(early), bits[-1])
    late = fold(late, after(l2, early))
    for bit in bits[2:-1]:
        late = fold(late, swap(upper(late), bit))
    l3 = swap(upper(late), bits[-1])
    widen_grad = fold(widen_grad, after(w3, late))
    widen_grad = add_x(widen_grad[0])
    early, late = fold(early, e3)[0], fold(late, l3)[0]
    narrow_grad = (narrow_grad.astype(F32) + n4.astype(F32)).astype(BF)
    narrow_grad = jnp.where(owner, narrow_grad, swap_core(narrow_grad))
    widen_grad = ordered(cb, widen_grad, swap_core(widen_grad), 1)
    input_grad = grad_one + back_own + back_recv[0].astype(F32) + back_far.astype(F32)

    mixer_grad = add_x(early[:, :half_width])
    mixer_grad = ordered(cb, mixer_grad, swap_core(mixer_grad), 1)
    mine = jnp.concatenate([early[:, half_width:], late], 1)
    theirs = swap_x(mine)
    qkv_grad, sums = place_qkv(place, mine, theirs, swap_core(mine), swap_core(theirs), width)
    return (
        result,
        input_grad,
        qkv_grad,
        mixer_grad.astype(F32),
        widen_grad.astype(F32),
        narrow_grad.astype(F32),
        sums[:, 0],
        sums[:, 1],
        sums[:, 2],
        sums[:, 3],
    )


def solution(mesh):
    placed = (
        P(("shard", "seq"), None),
        P("shard", None),
        P("shard", None),
        P("shard", None),
        P("shard", None),
        P("shard", None),
        P("shard"),
        P("shard"),
        P("shard"),
        P("shard"),
        P(("shard", "seq"), None),
    )
    return jax.shard_map(
        partial(shards, mesh.shape["shard"]),
        mesh=mesh,
        in_specs=placed,
        out_specs=(
            P(("shard", "seq"), None),
            P(("shard", "seq"), None),
            P("shard", None),
            P("shard", None),
            P("shard", None),
            P("shard", None),
            P("shard"),
            P("shard"),
            P("shard"),
            P("shard"),
        ),
        check_vma=False,
    )
```

time: 492 us -> 309 us (0.63)
  waiting for transfers between devices: 192 us -> 100 us
  matrix products: 35.2 us -> 1.02 us
  starting transfers between devices: 81.8 us -> 50.1 us
  other arithmetic: 45.1 us -> 14.5 us
  Pallas kernels: 109 us -> 116 us
    ppermute x38 -> x24, waiting for transfers between devices: 155 us -> 81.6 us  [swap(): return lax.ppermute(value, 'shard', [(i, i ^ mask) for i in range(n_shard)])]
    dot_general x18 -> x1, matrix products: 35.2 us -> 1.02 us  [dot(): lax.dot_general(a, b, (((ca,), (cb,)), ((), ())), preferred_element_type=...]
    ppermute x17 -> x10, waiting for transfers between devices: 31.4 us -> 8.46 us  [swap_x(): return lax.ppermute(value, 'seq', [(i, i ^ 2) for i in range(4)])]
    ppermute x38 -> x24, starting transfers between devices: 52.8 us -> 34.2 us  [swap(): return lax.ppermute(value, 'shard', [(i, i ^ mask) for i in range(n_shard)])]
    select_n x56 -> x5, other arithmetic: 13.6 us -> 2.4 us  [the longest x1 1.64 us: ordered(): jnp.where(flag == 0, jnp.concatenate([own, other], axis), jnp.concatenate...]
    unnamed x83 -> x114, local copies, waits for them, and re-layouts: 7.14 us -> 15.4 us
    ppermute x17 -> x10, starting transfers between devices: 19.3 us -> 11.3 us  [swap_x(): return lax.ppermute(value, 'seq', [(i, i ^ 2) for i in range(4)])]
    reduce_sum x7 -> x1, other arithmetic: 7.64 us -> 0.23 us  [shards(): begin = jnp.sum((ids[None] < first[:, None]).astype(jnp.int32), 1) // TILE]
  transfers between devices with their start and end apart: 72 -> 52, of which waited for: 32 -> 24; matrix products, arithmetic and copies ran while one was open for 12% -> 7% of each run, Pallas kernels for 23% -> 27%
where the time goes in v2:
time: 309 us; the launch traced here: 304 us
  Pallas kernels  116 us (38%)
  waiting for transfers between devices  100 us (32%)
  starting transfers between devices  50.1 us (16%)
  local copies, waits for them, and re-layouts  20.6 us (7%)
  other arithmetic  14.5 us (5%)
    ppermute x24, waiting for transfers between devices, swap(): return lax.ppermute(value, 'shard', [(i, i ^ mask) for i in range(n_shard)])  81.6 us
    pallas_call x3, Pallas kernels, attend_back(): pl.pallas_call(kernel, out_shape=(shape((TRIO, total), BF), shape((n_shar...  43.7 us
    ppermute x24, starting transfers between devices, swap(): return lax.ppermute(value, 'shard', [(i, i ^ mask) for i in range(n_shard)])  34.2 us
    pallas_call x3, Pallas kernels, attend(): pl.pallas_call(attend_kernel, out_shape=(shape((HEAD_DIM, half), BF), sha...  29.1 us
    unnamed x114, local copies, waits for them, and re-layouts  15.4 us
    ppermute x10, starting transfers between devices, swap_x(): return lax.ppermute(value, 'seq', [(i, i ^ 2) for i in range(4)])  11.3 us
    ppermute x10, waiting for transfers between devices, swap_x(): return lax.ppermute(value, 'seq', [(i, i ^ 2) for i in range(4)])  8.46 us
    ppermute x16, waiting for transfers between devices, swap_core(): return lax.ppermute(value, 'seq', [(i, i ^ 1) for i in range(4)])  7.68 us
  transfers between devices with their start and end apart: 52, of which 24 were waited for; matrix products, arithmetic and copies ran while one was open for 7% of the time, Pallas kernels for 27%

profile of v2, /device:TPU:0, one launch (start us, length us, event | category | flops | bytes accessed | tf_op | source)
XLA Modules:
  0.0 304.1 jit_solution(4515010564290428207)
XLA Ops:
  6.1 4.1 %collective-permute-start.3 = (bf16[1,96,256]{2,1,0:T(8,128)(2,1)S(1)}, bf16[1,96,256]{2,1,0:T(8,128)(2,1)S(1)}, u32[]{:S(2)}, u32[]{:S(2)}) collective-permute-start(bf16[1,96,256]{2,1,0:T(8,128)(2,1)S(1)} %bitcast.48), channel_id=1, source_target_pairs={{0,16},{4,20},{8,24},{12,28},{16,0},{20,4},{24,8},{28,12},{1,17},{... | collective-permute-start | bytes 147464 | tf_op jit(solution)/shard_map/ppermute | solution.py:750
  12.8 2.4 collective-permute-start.6
  17.4 5.4 %collective-permute-done.6 = bf16[1,96,768]{2,1,0:T(8,128)(2,1)S(1)} collective-permute-done((bf16[1,96,768]{2,1,0:T(8,128)(2,1)S(1)}, bf16[1,96,768]{2,1,0:T(8,128)(2,1)S(1)}, u32[]{:S(2)}, u32[]{:S(2)}) %collective-permute-start.6) | collective-permute-done | bytes 147488 | tf_op jit(solution)/shard_map/ppermute | solution.py:750
  26.4 4.9 %collective-permute-done.7 = bf16[2,96,768]{2,1,0:T(8,128)(2,1)S(1)} collective-permute-done((bf16[2,96,768]{2,1,0:T(8,128)(2,1)S(1)}, bf16[2,96,768]{2,1,0:T(8,128)(2,1)S(1)}, u32[]{:S(2)}, u32[]{:S(2)}) %collective-permute-start.7) | collective-permute-done | bytes 294944 | tf_op jit(solution)/shard_map/ppermute | solution.py:750
  35.6 10.5 %collective-permute-done.8.refs_1_ = bf16[4,96,768]{2,1,0:T(8,128)(2,1)} collective-permute-done((bf16[4,96,768]{2,1,0:T(8,128)(2,1)}, bf16[4,96,768]{2,1,0:T(8,128)(2,1)}, u32[]{:S(2)}, u32[]{:S(2)}) %collective-permute-start.8) | collective-permute-done | bytes 589856 | tf_op jit(solution)/shard_map/ppermute | solution.py:750
  55.9 9.8 %attend.3 = (bf16[64,1024]{1,0:T(8,128)(2,1)S(1)}, bf16[64,1024]{1,0:T(8,128)(2,1)S(1)}, f32[64,2048]{1,0:T(8,128)S(1)}, f32[1,2048]{1,0:T(1,128)S(1)}) custom-call(s32[10]{0:T(128)S(1)} %pad_add_fusion.info.refs_0_, bf16[512,768]{1,0:T(8,128)(2,1)S(1)} %copy-done.2, bf16[512,768]{1,0:T(8,128)(2,1)S(1)} %collective-permute-done.tok1.refs_2_, ...), custom_call_target="tpu_custom_call" | custom-call | flops 1 | bytes 1 | tf_op jit(solution)/shard_map/attend/pallas_call | solution.py:191
  67.0 3.2 %collective-permute-start.11 = (bf16[2,96,1536]{2,1,0:T(8,128)(2,1)S(1)}, bf16[2,96,1536]{2,1,0:T(8,128)(2,1)}, u32[]{:S(2)}, u32[]{:S(2)}) collective-permute-start(bf16[2,96,1536]{2,1,0:T(8,128)(2,1)S(1)} %pad_maximum_fusion.2.refs_0_), channel_id=1, source_target_pairs={{0,8},{4,12},{8,0},{12,4},{16,24},{20,28},{24,16},{28,20},{1,9},{5... | collective-permute-start | bytes 1769480 | tf_op jit(solution)/shard_map/ppermute | solution.py:750
  72.4 9.6 %attend.4 = (bf16[64,1024]{1,0:T(8,128)(2,1)S(1)}, bf16[64,1024]{1,0:T(8,128)(2,1)S(1)}, f32[64,2048]{1,0:T(8,128)S(1)}, f32[1,2048]{1,0:T(1,128)S(1)}) custom-call(s32[10]{0:T(128)S(1)} %pad_add_fusion.info.refs_0_, bf16[512,768]{1,0:T(8,128)(2,1)S(1)} %copy-done.2, bf16[512,768]{1,0:T(8,128)(2,1)S(1)} %collective-permute-done.tok1.refs_2_, ...), custom_call_target="tpu_custom_call" | custom-call | flops 1 | bytes 1 | tf_op jit(solution)/shard_map/attend/pallas_call | solution.py:191
  83.5 9.6 %attend.5 = (bf16[64,1024]{1,0:T(8,128)(2,1)S(1)}, bf16[64,1024]{1,0:T(8,128)(2,1)S(1)}, f32[64,2048]{1,0:T(8,128)S(1)}, f32[1,2048]{1,0:T(1,128)S(1)}) custom-call(s32[10]{0:T(128)S(1)} %pad_add_fusion.info.refs_0_, bf16[512,768]{1,0:T(8,128)(2,1)S(1)} %copy-done.2, bf16[512,768]{1,0:T(8,128)(2,1)S(1)} %collective-permute-done.tok1.refs_2_, ...), custom_call_target="tpu_custom_call" | custom-call | flops 1 | bytes 1 | tf_op jit(solution)/shard_map/attend/pallas_call | solution.py:191
  94.7 3.5 %collective-permute-done.14 = bf16[64,1024]{1,0:T(8,128)(2,1)S(1)} collective-permute-done((bf16[64,1024]{1,0:T(8,128)(2,1)S(1)}, bf16[64,1024]{1,0:T(8,128)(2,1)S(1)}, u32[]{:S(2)}, u32[]{:S(2)}) %collective-permute-start.14) | collective-permute-done | bytes 131104 | tf_op jit(solution)/shard_map/ppermute | solution.py:756
  107.5 3.0 first_norm.1
  112.3 6.6 %collective-permute-done.20.refs_1_ = bf16[1,384,768]{2,1,0:T(8,128)(2,1)} collective-permute-done((bf16[1,384,768]{2,1,0:T(8,128)(2,1)S(1)}, bf16[1,384,768]{2,1,0:T(8,128)(2,1)}, u32[]{:S(2)}, u32[]{:S(2)}) %collective-permute-start.20) | collective-permute-done | bytes 589856 | tf_op jit(solution)/shard_map/ppermute | solution.py:750
  125.4 6.9 %feed_up.1 = (bf16[1024,1536]{1,0:T(8,128)(2,1)S(1)}, bf16[1536,1024]{1,0:T(8,128)(2,1)S(1)}, bf16[1024,1536]{1,0:T(8,128)(2,1)S(1)}, bf16[768,1024]{1,0:T(8,128)(2,1)S(1)}) custom-call(bf16[512,768]{1,0:T(8,128)(2,1)} %get-tuple-element.112.low_own, bf16[512,768]{1,0:T(8,128)(2,1)} %collective-permute-done.17.low_other, bf16[768,1536]{1,0:T(8,128)(2,1)S(1)} %assemble.6.up), custom_call_target="tpu_custom_call" | custom-call | flops 1 | bytes 1 | tf_op jit(solution)/shard_map/feed_up/pallas_call | solution.py:424
  132.3 3.6 %collective-permute-done.22.refs_3_ = bf16[1,384,768]{2,1,0:T(8,128)(2,1)} collective-permute-done((bf16[1,384,768]{2,1,0:T(8,128)(2,1)}, bf16[1,384,768]{2,1,0:T(8,128)(2,1)}, u32[]{:S(2)}, u32[]{:S(2)}) %collective-permute-start.22) | collective-permute-done | bytes 589856 | tf_op jit(solution)/shard_map/ppermute | solution.py:750
  137.4 3.1 %feed_down.1 = (f32[512,768]{1,0:T(8,128)S(1)}, bf16[512,768]{1,0:T(8,128)(2,1)S(1)}) custom-call(bf16[1024,1536]{1,0:T(8,128)(2,1)S(1)} %get-tuple-element.115.act, bf16[1536,768]{1,0:T(8,128)(2,1)S(1)} %assemble.7.down), custom_call_target="tpu_custom_call" | custom-call | flops 1 | bytes 1 | tf_op jit(solution)/shard_map/feed_down/pallas_call | solution.py:457
  147.5 3.1 %weight_grad.2 = bf16[4,384,768]{2,1,0:T(8,128)(2,1)S(1)} custom-call(s32[1]{0:T(128)} %bitcast.14.info.refs_0_, bf16[1536,1024]{1,0:T(8,128)(2,1)S(1)} %get-tuple-element.125.refs_1_, bf16[512,768]{1,0:T(8,128)(2,1)S(1)} %get-tuple-element.126.refs_2_.grad_own, bf16[512,768]{1,0:T(8,128)(2,1)S(1)} %collective-permute-done.24.refs_3_.grad_other), custom_call_target="tpu_custom_call" | custom-call | flops 1 | bytes 1 | tf_op jit(solution)/shard_map/weight_grad/pallas_call | solution.py:536
  150.6 6.2 %feed_back.1 = (f32[512,768]{1,0:T(8,128)S(1)}, bf16[512,768]{1,0:T(8,128)(2,1)S(1)}, bf16[1024,1536]{1,0:T(8,128)(2,1)S(1)}) custom-call(bf16[512,768]{1,0:T(8,128)(2,1)S(1)} %get-tuple-element.126.refs_2_.grad_own, bf16[512,768]{1,0:T(8,128)(2,1)S(1)} %collective-permute-done.24.refs_3_.grad_other, bf16[1024,1536]{1,0:T(8,128)(2,1)S(1)} %get-tuple-element.127.slope, ...), custom_call_target="tpu_custom_call" | custom-call | flops 1 | bytes 1 | tf_op jit(solution)/shard_map/feed_back/pallas_call | solution.py:488
  166.5 3.5 %weight_grad.3 = bf16[8,96,1536]{2,1,0:T(8,128)(2,1)S(1)} custom-call(s32[1]{0:T(128)} %bitcast.4.info.refs_0_, bf16[768,1024]{1,0:T(8,128)(2,1)S(1)} %get-tuple-element.136.refs_1_, bf16[1024,1536]{1,0:T(8,128)(2,1)S(1)} %get-tuple-element.137.refs_2_), custom_call_target="tpu_custom_call" | custom-call | flops 1 | bytes 1 | tf_op jit(solution)/shard_map/weight_grad/pallas_call | solution.py:536
  171.3 14.7 %collective-permute-done.26 = bf16[2,384,768]{2,1,0:T(8,128)(2,1)S(1)} collective-permute-done((bf16[2,384,768]{2,1,0:T(8,128)(2,1)S(1)}, bf16[2,384,768]{2,1,0:T(8,128)(2,1)S(1)}, u32[]{:S(2)}, u32[]{:S(2)}) %collective-permute-start.26) | collective-permute-done | bytes 1179680 | tf_op jit(solution)/shard_map/ppermute | solution.py:750
  187.3 14.5 %attend_back.3 = (bf16[192,2048]{1,0:T(8,128)(2,1)S(1)}, bf16[8,96,256]{2,1,0:T(8,128)(2,1)S(1)}) custom-call(s32[10]{0:T(128)S(1)} %pad_add_fusion.info.refs_0_, bf16[512,768]{1,0:T(8,128)(2,1)S(1)} %copy-done.2, bf16[512,768]{1,0:T(8,128)(2,1)S(1)} %collective-permute-done.tok1.refs_2_, bf16[512,768]{1,0:T(8,128)(2,1)S(1)} %collective-permute-done.1.tok2.refs_3_, ...), custom_call_target="tpu_custom_call" | custom-call | flops 1 | bytes 1 | tf_op jit(solution)/shard_map/attend_back/pallas_call | solution.py:307
  203.5 14.7 %attend_back.4 = (bf16[192,2048]{1,0:T(8,128)(2,1)S(1)}, bf16[8,96,256]{2,1,0:T(8,128)(2,1)S(1)}) custom-call(s32[10]{0:T(128)S(1)} %pad_add_fusion.info.refs_0_, bf16[512,768]{1,0:T(8,128)(2,1)S(1)} %copy-done.2, bf16[512,768]{1,0:T(8,128)(2,1)S(1)} %collective-permute-done.tok1.refs_2_, bf16[512,768]{1,0:T(8,128)(2,1)S(1)} %collective-permute-done.1.tok2.refs_3_, ...), custom_call_target="tpu_custom_call" | custom-call | flops 1 | bytes 1 | tf_op jit(solution)/shard_map/attend_back/pallas_call | solution.py:307
  218.7 2.4 collective-permute-done.31
  221.3 14.5 %attend_back.5 = (bf16[192,2048]{1,0:T(8,128)(2,1)S(1)}, bf16[8,96,256]{2,1,0:T(8,128)(2,1)S(1)}) custom-call(s32[10]{0:T(128)S(1)} %pad_add_fusion.info.refs_0_, bf16[512,768]{1,0:T(8,128)(2,1)S(1)} %copy-done.2, bf16[512,768]{1,0:T(8,128)(2,1)S(1)} %collective-permute-done.tok1.refs_2_, bf16[512,768]{1,0:T(8,128)(2,1)S(1)} %collective-permute-done.1.tok2.refs_3_, ...), custom_call_target="tpu_custom_call" | custom-call | flops 1 | bytes 1 | tf_op jit(solution)/shard_map/attend_back/pallas_call | solution.py:307
  235.8 2.7 input_back.1
  242.4 12.0 %collective-permute-done.46 = bf16[2,96,1536]{2,1,0:T(8,128)(2,1)S(1)} collective-permute-done((bf16[2,96,1536]{2,1,0:T(8,128)(2,1)S(1)}, bf16[2,96,1536]{2,1,0:T(8,128)(2,1)S(1)}, u32[]{:S(2)}, u32[]{:S(2)}) %collective-permute-start.46) | collective-permute-done | bytes 589856 | tf_op jit(solution)/shard_map/ppermute | solution.py:750
  255.0 3.0 collective-permute-start.47
  263.9 11.3 %collective-permute-done.36 = bf16[2,96,896]{2,1,0:T(8,128)(2,1)S(1)} collective-permute-done((bf16[2,96,896]{2,1,0:T(8,128)(2,1)S(1)}, bf16[2,96,896]{2,1,0:T(8,128)(2,1)S(1)}, u32[]{:S(2)}, u32[]{:S(2)}) %collective-permute-start.36) | collective-permute-done | bytes 344096 | tf_op jit(solution)/shard_map/ppermute | solution.py:750
  276.7 2.7 collective-permute-start.38
  280.8 4.8 %collective-permute-done.40 = bf16[1,96,256]{2,1,0:T(8,128)(2,1)S(1)} collective-permute-done((bf16[1,96,256]{2,1,0:T(8,128)(2,1)S(1)}, bf16[1,96,256]{2,1,0:T(8,128)(2,1)S(1)}, u32[]{:S(2)}, u32[]{:S(2)}) %collective-permute-start.40) | collective-permute-done | bytes 49184 | tf_op jit(solution)/shard_map/ppermute | solution.py:750
  285.6 3.0 %collective-permute-done.38 = bf16[1,96,896]{2,1,0:T(8,128)(2,1)S(1)} collective-permute-done((bf16[1,96,896]{2,1,0:T(8,128)(2,1)S(1)}, bf16[1,96,896]{2,1,0:T(8,128)(2,1)S(1)}, u32[]{:S(2)}, u32[]{:S(2)}) %collective-permute-start.38) | collective-permute-done | bytes 172064 | tf_op jit(solution)/shard_map/ppermute | solution.py:750
  293.9 2.6 collective-permute-done.41.over_x
  298.8 3.0 place_qkv.1
  (275 shorter events, 96.9 us)
Async XLA Ops:
  10.2 24.3 %collective-permute-start.1 = (bf16[512,768]{1,0:T(8,128)(2,1)}, bf16[512,768]{1,0:T(8,128)(2,1)S(1)}, u32[]{:S(2)}, u32[]{:S(2)}) collective-permute-start(bf16[512,768]{1,0:T(8,128)(2,1)} %refs_1_.5), channel_id=1, source_target_pairs={{0,2},{1,3},{2,0},{3,1},{4,6},{5,7},{6,4},{7,5},{8,10},{9,11},{10,... | collective-permute-start | bytes 2359304 | tf_op jit(solution)/shard_map/ppermute | solution.py:756
  11.8 44.0 %collective-permute-start = (bf16[512,768]{1,0:T(8,128)(2,1)}, bf16[512,768]{1,0:T(8,128)(2,1)S(1)}, u32[]{:S(2)}, u32[]{:S(2)}) collective-permute-start(bf16[512,768]{1,0:T(8,128)(2,1)} %refs_1_.5), channel_id=1, source_target_pairs={{0,1},{1,0},{2,3},{3,2},{4,5},{5,4},{6,7},{7,6},{8,9},{9,8},{10,11... | collective-permute-start | bytes 2359304 | tf_op jit(solution)/shard_map/ppermute | solution.py:753
  12.8 10.0 %collective-permute-start.6 = (bf16[1,96,768]{2,1,0:T(8,128)(2,1)S(1)}, bf16[1,96,768]{2,1,0:T(8,128)(2,1)S(1)}, u32[]{:S(2)}, u32[]{:S(2)}) collective-permute-start(bf16[1,96,768]{2,1,0:T(8,128)(2,1)S(1)} %bitcast.45), channel_id=1, source_target_pairs={{0,16},{4,20},{8,24},{12,28},{16,0},{20,4},{24,8},{28,12},{1,17},{... | collective-permute-start | bytes 442376 | tf_op jit(solution)/shard_map/ppermute | solution.py:750
  32.1 14.0 %collective-permute-start.8 = (bf16[4,96,768]{2,1,0:T(8,128)(2,1)}, bf16[4,96,768]{2,1,0:T(8,128)(2,1)}, u32[]{:S(2)}, u32[]{:S(2)}) collective-permute-start(bf16[4,96,768]{2,1,0:T(8,128)(2,1)} %pad_maximum_fusion.1.refs_0_), channel_id=1, source_target_pairs={{0,4},{4,0},{8,12},{12,8},{16,20},{20,16},{24,28},{28,24},{1,5},{5... | collective-permute-start | bytes 1769480 | tf_op jit(solution)/shard_map/ppermute | solution.py:750
  34.5 21.3 %collective-permute-start.2 = (bf16[512,768]{1,0:T(8,128)(2,1)S(1)}, bf16[512,768]{1,0:T(8,128)(2,1)S(1)}, u32[]{:S(2)}, u32[]{:S(2)}) collective-permute-start(bf16[512,768]{1,0:T(8,128)(2,1)S(1)} %collective-permute-done.1.tok2.refs_3_), channel_id=1, source_target_pairs={{0,1},{1,0},{2,3},{3,2},{4,5},{5,4},{6,7},{7,6},{8,9},{9,8},{10,11... | collective-permute-start | bytes 2359304 | tf_op jit(solution)/shard_map/ppermute | solution.py:753
  34.6 16.7 %collective-permute-start.9 = (bf16[1,96,1536]{2,1,0:T(8,128)(2,1)}, bf16[1,96,1536]{2,1,0:T(8,128)(2,1)}, u32[]{:S(2)}, u32[]{:S(2)}) collective-permute-start(bf16[1,96,1536]{2,1,0:T(8,128)(2,1)} %dynamic-slice_bitcast_fusion), channel_id=1, source_target_pairs={{0,16},{4,20},{8,24},{12,28},{16,0},{20,4},{24,8},{28,12},{1,17},{... | collective-permute-start | bytes 884744 | tf_op jit(solution)/shard_map/ppermute | solution.py:750
  51.3 19.6 %collective-permute-start.10 = (bf16[384,768]{1,0:T(8,128)(2,1)}, bf16[384,768]{1,0:T(8,128)(2,1)S(1)}, u32[]{:S(2)}, u32[]{:S(2)}) collective-permute-start(bf16[384,768]{1,0:T(8,128)(2,1)} %param.16), channel_id=1, source_target_pairs={{0,16},{2,18},{4,20},{6,22},{8,24},{10,26},{12,28},{14,30},{17,1},... | collective-permute-start | bytes 1769480 | tf_op jit(solution)/shard_map/ppermute | solution.py:764
  67.0 16.3 %collective-permute-start.11 = (bf16[2,96,1536]{2,1,0:T(8,128)(2,1)S(1)}, bf16[2,96,1536]{2,1,0:T(8,128)(2,1)}, u32[]{:S(2)}, u32[]{:S(2)}) collective-permute-start(bf16[2,96,1536]{2,1,0:T(8,128)(2,1)S(1)} %pad_maximum_fusion.2.refs_0_), channel_id=1, source_target_pairs={{0,8},{4,12},{8,0},{12,4},{16,24},{20,28},{24,16},{28,20},{1,9},{5... | collective-permute-start | bytes 1769480 | tf_op jit(solution)/shard_map/ppermute | solution.py:750
  70.2 13.1 %collective-permute-start.18 = (bf16[2,96,1536]{2,1,0:T(8,128)(2,1)S(1)}, bf16[2,96,1536]{2,1,0:T(8,128)(2,1)S(1)}, u32[]{:S(2)}, u32[]{:S(2)}) collective-permute-start(bf16[2,96,1536]{2,1,0:T(8,128)(2,1)S(1)} %pad_maximum_fusion.2.refs_0_), channel_id=1, source_target_pairs={{0,4},{4,0},{8,12},{12,8},{16,20},{20,16},{24,28},{28,24},{1,5},{5... | collective-permute-start | bytes 1769480 | tf_op jit(solution)/shard_map/ppermute | solution.py:750
  71.0 23.6 %collective-permute-start.12 = (bf16[64,1024]{1,0:T(8,128)(2,1)S(1)}, bf16[64,1024]{1,0:T(8,128)(2,1)S(1)}, u32[]{:S(2)}, u32[]{:S(2)}) collective-permute-start(bf16[64,1024]{1,0:T(8,128)(2,1)S(1)} %get-tuple-element.108), channel_id=1, source_target_pairs={{0,2},{1,3},{2,0},{3,1},{4,6},{5,7},{6,4},{7,5},{8,10},{9,11},{10,... | collective-permute-start | bytes 393224 | tf_op jit(solution)/shard_map/ppermute | solution.py:756
  82.7 12.0 %collective-permute-start.13 = (bf16[64,1024]{1,0:T(8,128)(2,1)S(1)}, bf16[64,1024]{1,0:T(8,128)(2,1)S(1)}, u32[]{:S(2)}, u32[]{:S(2)}) collective-permute-start(bf16[64,1024]{1,0:T(8,128)(2,1)S(1)} %get-tuple-element.109), channel_id=1, source_target_pairs={{0,2},{1,3},{2,0},{3,1},{4,6},{5,7},{6,4},{7,5},{8,10},{9,11},{10,... | collective-permute-start | bytes 393224 | tf_op jit(solution)/shard_map/ppermute | solution.py:756
  83.4 21.3 %collective-permute-start.19 = (bf16[2,96,1536]{2,1,0:T(8,128)(2,1)}, bf16[2,96,1536]{2,1,0:T(8,128)(2,1)}, u32[]{:S(2)}, u32[]{:S(2)}) collective-permute-start(bf16[2,96,1536]{2,1,0:T(8,128)(2,1)} %collective-permute-done.11.refs_1_), channel_id=1, source_target_pairs={{0,4},{4,0},{8,12},{12,8},{16,20},{20,16},{24,28},{28,24},{1,5},{5... | collective-permute-start | bytes 1769480 | tf_op jit(solution)/shard_map/ppermute | solution.py:750
  103.0 15.9 %collective-permute-start.20 = (bf16[1,384,768]{2,1,0:T(8,128)(2,1)S(1)}, bf16[1,384,768]{2,1,0:T(8,128)(2,1)}, u32[]{:S(2)}, u32[]{:S(2)}) collective-permute-start(bf16[1,384,768]{2,1,0:T(8,128)(2,1)S(1)} %select_bitcast_fusion.refs_0_), channel_id=1, source_target_pairs={{0,8},{4,12},{8,0},{12,4},{16,24},{20,28},{24,16},{28,20},{1,9},{5... | collective-permute-start | bytes 1769480 | tf_op jit(solution)/shard_map/ppermute | solution.py:750
  104.7 15.5 %collective-permute-start.21 = (bf16[1,384,768]{2,1,0:T(8,128)(2,1)S(1)}, bf16[1,384,768]{2,1,0:T(8,128)(2,1)S(1)}, u32[]{:S(2)}, u32[]{:S(2)}) collective-permute-start(bf16[1,384,768]{2,1,0:T(8,128)(2,1)S(1)} %select_bitcast_fusion.refs_0_), channel_id=1, source_target_pairs={{0,4},{4,0},{8,12},{12,8},{16,20},{20,16},{24,28},{28,24},{1,5},{5... | collective-permute-start | bytes 1769480 | tf_op jit(solution)/shard_map/ppermute | solution.py:750
  112.3 13.1 %collective-permute-start.17 = (bf16[512,768]{1,0:T(8,128)(2,1)}, bf16[512,768]{1,0:T(8,128)(2,1)}, u32[]{:S(2)}, u32[]{:S(2)}) collective-permute-start(bf16[512,768]{1,0:T(8,128)(2,1)} %get-tuple-element.112.low_own), channel_id=1, source_target_pairs={{0,1},{1,0},{2,3},{3,2},{4,5},{5,4},{6,7},{7,6},{8,9},{9,8},{10,11... | collective-permute-start | bytes 2359304 | tf_op jit(solution)/shard_map/ppermute | solution.py:753
  121.0 15.0 %collective-permute-start.22 = (bf16[1,384,768]{2,1,0:T(8,128)(2,1)}, bf16[1,384,768]{2,1,0:T(8,128)(2,1)}, u32[]{:S(2)}, u32[]{:S(2)}) collective-permute-start(bf16[1,384,768]{2,1,0:T(8,128)(2,1)} %collective-permute-done.20.refs_1_), channel_id=1, source_target_pairs={{0,4},{4,0},{8,12},{12,8},{16,20},{20,16},{24,28},{28,24},{1,5},{5... | collective-permute-start | bytes 1769480 | tf_op jit(solution)/shard_map/ppermute | solution.py:750
  157.1 28.9 %collective-permute-start.26 = (bf16[2,384,768]{2,1,0:T(8,128)(2,1)S(1)}, bf16[2,384,768]{2,1,0:T(8,128)(2,1)S(1)}, u32[]{:S(2)}, u32[]{:S(2)}) collective-permute-start(bf16[2,384,768]{2,1,0:T(8,128)(2,1)S(1)} %slice.206), channel_id=1, source_target_pairs={{0,4},{4,0},{8,12},{12,8},{16,20},{20,16},{24,28},{28,24},{1,5},{5... | collective-permute-start | bytes 3538952 | tf_op jit(solution)/shard_map/ppermute | solution.py:750
  165.1 22.1 %collective-permute-start.29 = (bf16[192,1024]{1,0:T(8,128)(2,1)S(1)}, bf16[192,1024]{1,0:T(8,128)(2,1)S(1)}, u32[]{:S(2)}, u32[]{:S(2)}) collective-permute-start(bf16[192,1024]{1,0:T(8,128)(2,1)S(1)} %get-tuple-element.135), channel_id=1, source_target_pairs={{0,2},{1,3},{2,0},{3,1},{4,6},{5,7},{6,4},{7,5},{8,10},{9,11},{10,... | collective-permute-start | bytes 1179656 | tf_op jit(solution)/shard_map/ppermute | solution.py:756
  170.0 48.4 %collective-permute-start.32 = (bf16[4,96,1536]{2,1,0:T(8,128)(2,1)S(1)}, bf16[4,96,1536]{2,1,0:T(8,128)(2,1)S(1)}, u32[]{:S(2)}, u32[]{:S(2)}) collective-permute-start(bf16[4,96,1536]{2,1,0:T(8,128)(2,1)S(1)} %slice.212), channel_id=1, source_target_pairs={{0,4},{4,0},{8,12},{12,8},{16,20},{20,16},{24,28},{28,24},{1,5},{5... | collective-permute-start | bytes 3538952 | tf_op jit(solution)/shard_map/ppermute | solution.py:750
  186.3 15.5 %collective-permute-start.30 = (bf16[1,384,768]{2,1,0:T(8,128)(2,1)S(1)}, bf16[1,384,768]{2,1,0:T(8,128)(2,1)S(1)}, u32[]{:S(2)}, u32[]{:S(2)}) collective-permute-start(bf16[1,384,768]{2,1,0:T(8,128)(2,1)S(1)} %slice.209), channel_id=1, source_target_pairs={{0,8},{4,12},{8,0},{12,4},{16,24},{20,28},{24,16},{28,20},{1,9},{5... | collective-permute-start | bytes 1769480 | tf_op jit(solution)/shard_map/ppermute | solution.py:750
  202.0 19.1 %collective-permute-start.31 = (bf16[384,768]{1,0:T(8,128)(2,1)S(1)}, bf16[384,768]{1,0:T(8,128)(2,1)S(1)}, u32[]{:S(2)}, u32[]{:S(2)}) collective-permute-start(bf16[384,768]{1,0:T(8,128)(2,1)S(1)} %fusion.2), channel_id=1, source_target_pairs={{1,17},{3,19},{5,21},{7,23},{9,25},{11,27},{13,29},{15,31},{16,0},... | collective-permute-start | bytes 1769480 | tf_op jit(solution)/shard_map/ppermute | solution.py:764
  238.5 19.4 %collective-permute-start.33 = (bf16[2,512,768]{2,1,0:T(8,128)(2,1)S(1)}, bf16[2,512,768]{2,1,0:T(8,128)(2,1)S(1)}, u32[]{:S(2)}, u32[]{:S(2)}) collective-permute-start(bf16[2,512,768]{2,1,0:T(8,128)(2,1)S(1)} %get-tuple-element.161), channel_id=1, source_target_pairs={{0,1},{1,0},{2,3},{3,2},{4,5},{5,4},{6,7},{7,6},{8,9},{9,8},{10,11... | collective-permute-start | bytes 4718600 | tf_op jit(solution)/shard_map/ppermute | solution.py:753
  238.7 15.8 %collective-permute-start.46 = (bf16[2,96,1536]{2,1,0:T(8,128)(2,1)S(1)}, bf16[2,96,1536]{2,1,0:T(8,128)(2,1)S(1)}, u32[]{:S(2)}, u32[]{:S(2)}) collective-permute-start(bf16[2,96,1536]{2,1,0:T(8,128)(2,1)S(1)} %slice.229), channel_id=1, source_target_pairs={{0,8},{4,12},{8,0},{12,4},{16,24},{20,28},{24,16},{28,20},{1,9},{5... | collective-permute-start | bytes 1769480 | tf_op jit(solution)/shard_map/ppermute | solution.py:750
  239.6 15.0 %collective-permute-start.50 = (bf16[384,768]{1,0:T(8,128)(2,1)S(1)}, bf16[384,768]{1,0:T(8,128)(2,1)S(1)}, u32[]{:S(2)}, u32[]{:S(2)}) collective-permute-start(bf16[384,768]{1,0:T(8,128)(2,1)S(1)} %add_convert_fusion.5), channel_id=1, source_target_pairs={{0,2},{1,3},{2,0},{3,1},{4,6},{5,7},{6,4},{7,5},{8,10},{9,11},{10,... | collective-permute-start | bytes 1769480 | tf_op jit(solution)/shard_map/ppermute | solution.py:756
  240.3 18.3 %collective-permute-start.35 = (bf16[4,96,896]{2,1,0:T(8,128)(2,1)S(1)}, bf16[4,96,896]{2,1,0:T(8,128)(2,1)S(1)}, u32[]{:S(2)}, u32[]{:S(2)}) collective-permute-start(bf16[4,96,896]{2,1,0:T(8,128)(2,1)S(1)} %slice.217), channel_id=1, source_target_pairs={{0,4},{4,0},{8,12},{12,8},{16,20},{20,16},{24,28},{28,24},{1,5},{5... | collective-permute-start | bytes 2064392 | tf_op jit(solution)/shard_map/ppermute | solution.py:750
  241.7 20.8 %collective-permute-start.37 = (bf16[4,96,256]{2,1,0:T(8,128)(2,1)S(1)}, bf16[4,96,256]{2,1,0:T(8,128)(2,1)S(1)}, u32[]{:S(2)}, u32[]{:S(2)}) collective-permute-start(bf16[4,96,256]{2,1,0:T(8,128)(2,1)S(1)} %slice.178), channel_id=1, source_target_pairs={{0,4},{4,0},{8,12},{12,8},{16,20},{20,16},{24,28},{28,24},{1,5},{5... | collective-permute-start | bytes 589832 | tf_op jit(solution)/shard_map/ppermute | solution.py:750
  255.0 21.3 %collective-permute-start.47 = (bf16[1,96,1536]{2,1,0:T(8,128)(2,1)S(1)}, bf16[1,96,1536]{2,1,0:T(8,128)(2,1)S(1)}, u32[]{:S(2)}, u32[]{:S(2)}) collective-permute-start(bf16[1,96,1536]{2,1,0:T(8,128)(2,1)S(1)} %slice.231), channel_id=1, source_target_pairs={{0,16},{4,20},{8,24},{12,28},{16,0},{20,4},{24,8},{28,12},{1,17},{... | collective-permute-start | bytes 884744 | tf_op jit(solution)/shard_map/ppermute | solution.py:750
  258.8 16.3 %collective-permute-start.36 = (bf16[2,96,896]{2,1,0:T(8,128)(2,1)S(1)}, bf16[2,96,896]{2,1,0:T(8,128)(2,1)S(1)}, u32[]{:S(2)}, u32[]{:S(2)}) collective-permute-start(bf16[2,96,896]{2,1,0:T(8,128)(2,1)S(1)} %slice.219), channel_id=1, source_target_pairs={{0,8},{4,12},{8,0},{12,4},{16,24},{20,28},{24,16},{28,20},{1,9},{5... | collective-permute-start | bytes 1032200 | tf_op jit(solution)/shard_map/ppermute | solution.py:750
  261.9 35.3 %collective-permute-start.34 = (bf16[512,768]{1,0:T(8,128)(2,1)S(1)}, bf16[512,768]{1,0:T(8,128)(2,1)S(1)}, u32[]{:S(2)}, u32[]{:S(2)}) collective-permute-start(bf16[512,768]{1,0:T(8,128)(2,1)S(1)} %fusion), channel_id=1, source_target_pairs={{0,2},{1,3},{2,0},{3,1},{4,6},{5,7},{6,4},{7,5},{8,10},{9,11},{10,... | collective-permute-start | bytes 2359304 | tf_op jit(solution)/shard_map/ppermute | solution.py:756
  262.7 13.6 %collective-permute-start.39 = (bf16[2,96,256]{2,1,0:T(8,128)(2,1)S(1)}, bf16[2,96,256]{2,1,0:T(8,128)(2,1)S(1)}, u32[]{:S(2)}, u32[]{:S(2)}) collective-permute-start(bf16[2,96,256]{2,1,0:T(8,128)(2,1)S(1)} %slice.224), channel_id=1, source_target_pairs={{0,8},{4,12},{8,0},{12,4},{16,24},{20,28},{24,16},{28,20},{1,9},{5... | collective-permute-start | bytes 294920 | tf_op jit(solution)/shard_map/ppermute | solution.py:750
  276.7 11.9 %collective-permute-start.38 = (bf16[1,96,896]{2,1,0:T(8,128)(2,1)S(1)}, bf16[1,96,896]{2,1,0:T(8,128)(2,1)S(1)}, u32[]{:S(2)}, u32[]{:S(2)}) collective-permute-start(bf16[1,96,896]{2,1,0:T(8,128)(2,1)S(1)} %slice.221), channel_id=1, source_target_pairs={{0,16},{4,20},{8,24},{12,28},{16,0},{20,4},{24,8},{28,12},{1,17},{... | collective-permute-start | bytes 516104 | tf_op jit(solution)/shard_map/ppermute | solution.py:750
  279.4 13.8 %collective-permute-start.48 = (bf16[96,1536]{1,0:T(8,128)(2,1)S(1)}, bf16[96,1536]{1,0:T(8,128)(2,1)S(1)}, u32[]{:S(2)}, u32[]{:S(2)}) collective-permute-start(bf16[96,1536]{1,0:T(8,128)(2,1)S(1)} %fusion.4), channel_id=1, source_target_pairs={{0,2},{1,3},{2,0},{3,1},{4,6},{5,7},{6,4},{7,5},{8,10},{9,11},{10,... | collective-permute-start | bytes 884744 | tf_op jit(solution)/shard_map/ppermute | solution.py:756
  (73 other events, 424.4 us)
